TPU v7x, 128 devices: a whole 4x4x4 slice. The times are simulated.
128 devices in a mesh: expert: 64 (over x, z, y), replica: 2 (over core).
Axes of the slice: x: 4, y: 4, z: 4, core: 2. Of those that a mesh axis runs over, the one named last changes fastest.
Arguments:
- tokens: bfloat16 [65536, 1024], P(('expert', 'replica')), may hold values from -6 to 6
- expert_id: int32 [65536, 1], P(('expert', 'replica')), may hold values from 0 to 63; in each aligned block of 512 rows (0 to 511, 512 to 1023, ...) at most 16 rows name the same one
- router_prob: float32 [65536], P(('expert', 'replica')), may hold values from 0.1 to 1
- keep_mask: int32 [64, 128, 2048], P('expert'), may hold values 0 or 1
- w_in: bfloat16 [64, 1024, 2048], P('expert'), may hold values from -0.1875 to 0.1875
- w_out: bfloat16 [64, 2048, 1024], P('expert'), may hold values from -0.125 to 0.125
- cotangent: bfloat16 [65536, 1024], P(('expert', 'replica')), may hold values from -0.59765625 to 0.59765625
Outputs:
- mixed: bfloat16 [65536, 1024], P(('expert', 'replica'))
- grad_in: float32 [64, 1024, 2048], P('expert', 'replica')
- grad_out: float32 [64, 2048, 1024], P('expert', 'replica')
Inputs may be any that keep to these rules, and one draw needn't show every extreme that they name: `expert_id`: among the 512 tokens of one device no expert is chosen more than 16 times; on some devices one expert is chosen exactly 16 times.
All inputs are finite; a program needn't handle non-finite values. No bound on the sum of `keep_mask` on one device may be relied on, other than what follows from the above.
Results may differ from a plain program's by a relative error of at most 0.0057.
Values may be sent and summed in bfloat16 or wider, within the bound.
No kernel may reach another device: no remote copies, remote signals or barrier semaphores. Data moves between devices by JAX's collectives and lax.ppermute only.
A program may use at most 128 MiB of HBM per device.

v0:
```python
import jax
import jax.numpy as jnp
from jax import lax
from jax.sharding import PartitionSpec as P

KEEP_SCALE = 4.0 / 3.0
SWAP = [(0, 1), (1, 0)]


def gelu_parts(pre):
    inner = 0.7978845608 * (pre + 0.044715 * pre * pre * pre)
    tanh_v = jnp.tanh(inner)
    value = 0.5 * pre * (1.0 + tanh_v)
    slope = 0.5 * (1.0 + tanh_v) + 0.5 * pre * (1.0 - tanh_v * tanh_v) * 0.7978845608 * (
        1.0 + 3.0 * 0.044715 * pre * pre
    )
    return (value, slope)


def exchange(array):
    return lax.all_to_all(array, "expert", split_axis=0, concat_axis=0, tiled=True)


def summed_over_copies(rows, columns):
    half = rows.shape[1] // 2
    here = lax.axis_index("replica")

    def product(which):
        part = lax.dynamic_slice_in_dim(rows, which * half, half, axis=1)
        return lax.dot_general(
            part, columns, (((0,), (0,)), ((), ())), preferred_element_type=jnp.float32
        )

    other = lax.ppermute(product(1 - here).astype(jnp.bfloat16), "replica", SWAP)
    return product(here) + other.astype(jnp.float32)


def shards(tokens, expert_id, router_prob, keep_mask, w_in, w_out, cotangent):
    tok_rows, width = tokens.shape
    n_expert = lax.axis_size("expert")
    n_replica = lax.axis_size("replica")
    capacity = 2 * tok_rows // n_expert
    slots = n_expert * capacity
    weight_in = w_in[0]
    weight_out = w_out[0]
    ids = expert_id[:, 0]
    order = jnp.arange(tok_rows, dtype=jnp.int32)
    earlier = (ids[:, None] == ids[None, :]) & (order[None, :] < order[:, None])
    ranks = jnp.sum(earlier.astype(jnp.int32), axis=1)
    target = ids * capacity + ranks
    select = (target[:, None] == jnp.arange(slots, dtype=jnp.int32)[None, :]).astype(jnp.bfloat16)

    def fill_slots(values):
        filled = lax.dot_general(
            select, values, (((0,), (0,)), ((), ())), preferred_element_type=jnp.float32
        )
        return filled.astype(jnp.bfloat16).reshape(n_expert, capacity, width)

    received = exchange(fill_slots(tokens)).reshape(slots, width)
    gated = (router_prob[:, None] * cotangent.astype(jnp.float32)).astype(jnp.bfloat16)
    grad_rows = exchange(fill_slots(gated)).reshape(slots, width)
    keep_rows = lax.dynamic_index_in_dim(
        keep_mask[0].reshape(n_expert, n_replica, -1),
        lax.axis_index("replica"),
        axis=1,
        keepdims=False,
    )
    keep_scale = keep_rows.astype(jnp.float32) * KEEP_SCALE
    keep_scale = jnp.broadcast_to(keep_scale[:, None, :], (n_expert, capacity, keep_scale.shape[1]))
    keep_scale = keep_scale.reshape(slots, -1)
    pre = jnp.dot(received, weight_in, preferred_element_type=jnp.float32)
    value, slope = gelu_parts(pre)
    hidden = (value * keep_scale).astype(jnp.bfloat16)
    slope = slope * keep_scale
    out = jnp.dot(hidden, weight_out, preferred_element_type=jnp.float32).astype(jnp.bfloat16)
    back = exchange(out.reshape(n_expert, capacity, width)).reshape(slots, width)
    grad_out = summed_over_copies(hidden, grad_rows)
    dhidden = lax.dot_general(
        grad_rows, weight_out, (((1,), (1,)), ((), ())), preferred_element_type=jnp.float32
    )
    dpre = (dhidden * slope).astype(jnp.bfloat16)
    grad_in = summed_over_copies(received, dpre)
    expert_out = jnp.dot(select, back, preferred_element_type=jnp.float32)
    mixed = (router_prob[:, None] * expert_out).astype(jnp.bfloat16)
    return (mixed, grad_in[None], grad_out[None])


def solution(mesh):
    in_specs = (
        P(("expert", "replica"), None),
        P(("expert", "replica"), None),
        P(("expert", "replica")),
        P("expert", None, None),
        P("expert", None, None),
        P("expert", None, None),
        P(("expert", "replica"), None),
    )
    out_specs = (
        P(("expert", "replica"), None),
        P("expert", "replica", None),
        P("expert", "replica", None),
    )
    return jax.shard_map(shards, mesh=mesh, in_specs=in_specs, out_specs=out_specs, check_vma=False)
```

profile of v0, /device:TPU:0, one launch (start us, length us, event | category | flops | bytes accessed | tf_op | source)
XLA Modules:
  0.0 133.5 jit_solution(17687601367994418590)
XLA Ops:
  0.6 0.0 copy-start
  0.6 1.0 convert_reduce_fusion
  1.7 0.7 multiply_add_fusion.1
  2.4 2.7 %fusion.22 = bf16[1024,1024]{1,0:T(8,128)(2,1)} fusion(bf16[512,1024]{1,0:T(8,128)(2,1)S(1)} %copy-done, s32[512]{0:T(512)S(1)} %bitcast.56), kind=kOutput, calls=%fused_computation.30 | convolution fusion | flops 1075314688 | bytes 3147776 | tf_op jit(solution)/shard_map/dot_general | solution.py:54
  5.1 11.6 %all-to-all-start = ((bf16[64,16,1024]{2,1,0:T(8,128)(2,1)}), bf16[64,16,1024]{2,1,0:T(8,128)(2,1)S(1)}, u32[]{:S(2)}, u32[]{:S(2)}) async-start(bf16[64,16,1024]{2,1,0:T(8,128)(2,1)} %bitcast.53), calls=%async_computation | async-start | bytes 4194304 | tf_op jit(solution)/shard_map/all_to_all | solution.py:21
  16.7 4.0 %fusion.23 = bf16[1024,1024]{1,0:T(8,128)(2,1)} fusion(bf16[512,1024]{1,0:T(8,128)(2,1)} %param.13, s32[512]{0:T(512)S(1)} %bitcast.57, f32[512]{0:T(512)S(1)} %copy-done.6), kind=kOutput, calls=%fused_computation.31 | convolution fusion | flops 1076887552 | bytes 3149824 | tf_op jit(solution)/shard_map/dot_general | solution.py:54
  20.7 25.6 %all-to-all-done = bf16[64,16,1024]{2,1,0:T(8,128)(2,1)S(1)} async-done(((bf16[64,16,1024]{2,1,0:T(8,128)(2,1)}), bf16[64,16,1024]{2,1,0:T(8,128)(2,1)S(1)}, u32[]{:S(2)}, u32[]{:S(2)}) %all-to-all-start) | async-done | bytes 2097184 | tf_op jit(solution)/shard_map/all_to_all | solution.py:21
  46.3 5.6 %all-to-all-start.2 = ((bf16[64,16,1024]{2,1,0:T(8,128)(2,1)}), bf16[64,16,1024]{2,1,0:T(8,128)(2,1)}, u32[]{:S(2)}, u32[]{:S(2)}) async-start(bf16[64,16,1024]{2,1,0:T(8,128)(2,1)} %bitcast.52), calls=%async_computation.2 | async-start | bytes 4194304 | tf_op jit(solution)/shard_map/all_to_all | solution.py:21
  51.9 2.8 %reshape_squeeze.3 = s32[64,2,2048]{2,1,0:T(2,128)} reshape(s32[1,128,2048]{2,1,0:T(8,128)} %param.10) | data formatting | bytes 2097152 | tf_op jit(solution)/shard_map/reshape;squeeze | solution.py:63
  54.7 1.9 %convert_multiply_fusion = f32[64,1,2048]{2,1,0:T(1,128)S(1)} fusion(s32[64,2,2048]{2,1,0:T(2,128)} %reshape_squeeze.3, s32[]{:T(128)S(6)} %select_n.16), kind=kLoop, calls=%fused_computation.45 | loop fusion | flops 262144 | bytes 1048580 | tf_op jit(solution)/shard_map/mul | solution.py:68
  56.6 1.0 copy.12
  57.5 10.9 %fusion.5 = (bf16[1024,2048]{1,0:T(8,128)(2,1)S(1)}, f32[1024,2048]{1,0:T(8,128)}) fusion(f32[64,2048]{1,0:T(8,128)} %bitcast.49, bf16[1024,1024]{1,0:T(8,128)(2,1)S(1)} %bitcast.46, bf16[1,1024,2048]{2,1,0:T(8,128)(2,1)} %param.11), kind=kOutput, calls=%fused_computation.9 | convolution fusion | flops 4315938816 | bytes 19398656 | tf_op jit(solution)/shard_map/dot_general | solution.py:71
  68.4 2.0 %copy-done.4 = bf16[1024,2048]{1,0:T(8,128)(2,1)} copy-done((bf16[1024,2048]{1,0:T(8,128)(2,1)}, bf16[1024,2048]{1,0:T(8,128)(2,1)S(1)}, u32[]{:S(2)}) %copy-start.4) | copy-done | bytes 4194328
  70.4 5.7 %fusion.27 = bf16[1024,1024]{1,0:T(8,128)(2,1)} fusion(bf16[1024,2048]{1,0:T(8,128)(2,1)S(1)} %get-tuple-element.3, bf16[1,2048,1024]{2,1,0:T(8,128)(2,1)S(1)} %copy-done.3), kind=kOutput, calls=%fused_computation.33 | convolution fusion | flops 4296015872 | bytes 10485760 | tf_op jit(solution)/shard_map/dot_general | solution.py:75
  76.1 4.7 %all-to-all-done.2 = bf16[64,16,1024]{2,1,0:T(8,128)(2,1)} async-done(((bf16[64,16,1024]{2,1,0:T(8,128)(2,1)}), bf16[64,16,1024]{2,1,0:T(8,128)(2,1)}, u32[]{:S(2)}, u32[]{:S(2)}) %all-to-all-start.2) | async-done | bytes 2097184 | tf_op jit(solution)/shard_map/all_to_all | solution.py:21
  80.8 6.4 %all-to-all-start.1 = ((bf16[64,16,1024]{2,1,0:T(8,128)(2,1)}), bf16[64,16,1024]{2,1,0:T(8,128)(2,1)}, u32[]{:S(2)}, u32[]{:S(2)}) async-start(bf16[64,16,1024]{2,1,0:T(8,128)(2,1)} %bitcast.51), calls=%async_computation.1 | async-start | bytes 4194304 | tf_op jit(solution)/shard_map/all_to_all | solution.py:21
  87.2 5.9 %fusion.24 = bf16[1024,1024]{1,0:T(8,128)(2,1)} fusion(bf16[1024,1024]{1,0:T(8,128)(2,1)} %bitcast.11, bf16[1024,2048]{1,0:T(8,128)(2,1)} %copy-done.4, s32[]{:T(128)S(6)} %select_n.20), kind=kOutput, calls=%fused_computation.32 | convolution fusion | flops 2148532224 | bytes 6291460 | tf_op jit(solution)/shard_map/dot_general | solution.py:30
  93.1 13.6 %fusion.7 = bf16[1024,2048]{1,0:T(8,128)(2,1)S(1)} fusion(f32[1024,2048]{1,0:T(8,128)} %get-tuple-element.4, bf16[1024,1024]{1,0:T(8,128)(2,1)} %bitcast.11, bf16[1,2048,1024]{2,1,0:T(8,128)(2,1)} %param.12, f32[64,2048]{1,0:T(8,128)} %bitcast.50), kind=kOutput, calls=%fused_computation.11 | convolution fusion | flops 4336910336 | bytes 19398656 | tf_op jit(solution)/shard_map/dot_general | solution.py:78
  106.8 3.7 %convolution_convert_fusion = bf16[512,2048]{1,0:T(8,128)(2,1)} fusion(bf16[1024,2048]{1,0:T(8,128)(2,1)S(1)} %fusion.7, bf16[1024,1024]{1,0:T(8,128)(2,1)S(1)} %bitcast.47, s32[]{:T(128)S(6)} %select_n.18), kind=kOutput, calls=%fused_computation.19 | convolution fusion | flops 2148532224 | bytes 7340036 | tf_op jit(solution)/shard_map/dot_general | solution.py:30
  110.5 0.5 collective-permute-start
  111.0 5.5 %all-to-all-done.1 = bf16[64,16,1024]{2,1,0:T(8,128)(2,1)} async-done(((bf16[64,16,1024]{2,1,0:T(8,128)(2,1)}), bf16[64,16,1024]{2,1,0:T(8,128)(2,1)}, u32[]{:S(2)}, u32[]{:S(2)}) %all-to-all-start.1) | async-done | bytes 2097184 | tf_op jit(solution)/shard_map/all_to_all | solution.py:21
  116.5 4.0 %multiply_convert_fusion.1 = bf16[512,1024]{1,0:T(8,128)(2,1)} fusion(bf16[1024,1024]{1,0:T(8,128)(2,1)} %bitcast.9, s32[512]{0:T(512)S(1)} %bitcast.58, f32[512]{0:T(512)S(1)} %copy-done.6), kind=kOutput, calls=%fused_computation.25 | convolution fusion | flops 1075314688 | bytes 3149824 | tf_op jit(solution)/shard_map/dot_general | solution.py:83
  120.6 6.9 %add_bitcast_fusion = f32[1,1024,1024]{2,1,0:T(8,128)} fusion(bf16[1024,1024]{1,0:T(8,128)(2,1)} %collective-permute-done.1, bf16[1024,1024]{1,0:T(8,128)(2,1)} %bitcast.11, bf16[1024,2048]{1,0:T(8,128)(2,1)S(1)} %copy-done.5, s32[]{:T(128)S(6)} %select_n.19), kind=kOutput, calls=%fused_computation.17 | convolution fusion | flops 2149580800 | bytes 10485764 | tf_op jit(solution)/shard_map/dot_general | solution.py:30
  127.4 6.1 %add_bitcast_fusion.1 = f32[1,512,2048]{2,1,0:T(8,128)} fusion(bf16[512,2048]{1,0:T(8,128)(2,1)} %collective-permute-done, bf16[1024,2048]{1,0:T(8,128)(2,1)S(1)} %copy-done.2, bf16[1024,1024]{1,0:T(8,128)(2,1)S(1)} %bitcast.48, s32[]{:T(128)S(6)} %select_n.17), kind=kOutput, calls=%fused_computation.18 | convolution fusion | flops 2149580800 | bytes 11534340 | tf_op jit(solution)/shard_map/dot_general | solution.py:30
  (15 shorter events, 0.0 us)
Async XLA Ops:
  0.6 1.7 %copy-start = (bf16[512,1024]{1,0:T(8,128)(2,1)S(1)}, bf16[512,1024]{1,0:T(8,128)(2,1)}, u32[]{:S(2)}) copy-start(bf16[512,1024]{1,0:T(8,128)(2,1)} %param.7) | copy-start | bytes 3145732
  5.1 11.6 %copy-start.6 = (f32[512]{0:T(512)S(1)}, f32[512]{0:T(512)}, u32[]{:S(2)}) copy-start(f32[512]{0:T(512)} %param.9) | copy-start | bytes 6148
  5.1 41.2 %all-to-all-start = ((bf16[64,16,1024]{2,1,0:T(8,128)(2,1)}), bf16[64,16,1024]{2,1,0:T(8,128)(2,1)S(1)}, u32[]{:S(2)}, u32[]{:S(2)}) async-start(bf16[64,16,1024]{2,1,0:T(8,128)(2,1)} %bitcast.53), calls=%async_computation | async-start | bytes 4194304 | tf_op jit(solution)/shard_map/all_to_all | solution.py:21
  46.3 34.5 %all-to-all-start.2 = ((bf16[64,16,1024]{2,1,0:T(8,128)(2,1)}), bf16[64,16,1024]{2,1,0:T(8,128)(2,1)}, u32[]{:S(2)}, u32[]{:S(2)}) async-start(bf16[64,16,1024]{2,1,0:T(8,128)(2,1)} %bitcast.52), calls=%async_computation.2 | async-start | bytes 4194304 | tf_op jit(solution)/shard_map/all_to_all | solution.py:21
  57.5 12.9 %copy-start.3 = (bf16[1,2048,1024]{2,1,0:T(8,128)(2,1)S(1)}, bf16[1,2048,1024]{2,1,0:T(8,128)(2,1)}, u32[]{:S(2)}) copy-start(bf16[1,2048,1024]{2,1,0:T(8,128)(2,1)} %param.12) | copy-start | bytes 12582916
  68.4 2.0 %copy-start.4 = (bf16[1024,2048]{1,0:T(8,128)(2,1)}, bf16[1024,2048]{1,0:T(8,128)(2,1)S(1)}, u32[]{:S(2)}) copy-start(bf16[1024,2048]{1,0:T(8,128)(2,1)S(1)} %get-tuple-element.3) | copy-start | bytes 12582916
  80.8 35.7 %all-to-all-start.1 = ((bf16[64,16,1024]{2,1,0:T(8,128)(2,1)}), bf16[64,16,1024]{2,1,0:T(8,128)(2,1)}, u32[]{:S(2)}, u32[]{:S(2)}) async-start(bf16[64,16,1024]{2,1,0:T(8,128)(2,1)} %bitcast.51), calls=%async_computation.1 | async-start | bytes 4194304 | tf_op jit(solution)/shard_map/all_to_all | solution.py:21
  93.1 27.4 %collective-permute-start.1 = (bf16[1024,1024]{1,0:T(8,128)(2,1)}, bf16[1024,1024]{1,0:T(8,128)(2,1)}, u32[]{:S(2)}, u32[]{:S(2)}) collective-permute-start(bf16[1024,1024]{1,0:T(8,128)(2,1)} %fusion.24), channel_id=1, source_target_pairs={{0,1},{1,0},{2,3},{3,2},{4,5},{5,4},{6,7},{7,6},{8,9},{9,8},{10,11... | collective-permute-start | bytes 6291464 | tf_op jit(solution)/shard_map/ppermute | solution.py:34
  106.8 3.8 %copy-start.1 = (bf16[1024,2048]{1,0:T(8,128)(2,1)}, bf16[1024,2048]{1,0:T(8,128)(2,1)S(1)}, u32[]{:S(2)}) copy-start(bf16[1024,2048]{1,0:T(8,128)(2,1)S(1)} %fusion.7) | copy-start | bytes 12582916
  110.5 16.9 %collective-permute-start = (bf16[512,2048]{1,0:T(8,128)(2,1)}, bf16[512,2048]{1,0:T(8,128)(2,1)}, u32[]{:S(2)}, u32[]{:S(2)}) collective-permute-start(bf16[512,2048]{1,0:T(8,128)(2,1)} %convolution_convert_fusion), channel_id=1, source_target_pairs={{0,1},{1,0},{2,3},{3,2},{4,5},{5,4},{6,7},{7,6},{8,9},{9,8},{10,11... | collective-permute-start | bytes 6291464 | tf_op jit(solution)/shard_map/ppermute | solution.py:34
  116.5 4.0 %copy-start.5 = (bf16[1024,2048]{1,0:T(8,128)(2,1)S(1)}, bf16[1024,2048]{1,0:T(8,128)(2,1)}, u32[]{:S(2)}) copy-start(bf16[1024,2048]{1,0:T(8,128)(2,1)} %copy-done.4) | copy-start | bytes 12582916
  120.5 6.9 %copy-start.2 = (bf16[1024,2048]{1,0:T(8,128)(2,1)S(1)}, bf16[1024,2048]{1,0:T(8,128)(2,1)}, u32[]{:S(2)}) copy-start(bf16[1024,2048]{1,0:T(8,128)(2,1)} %copy-done.1) | copy-start | bytes 12582916
where the time goes:
time: 134 us; the launch traced here: 133 us
  matrix products  63.5 us (47%)
  waiting for transfers between devices  35.8 us (27%)
  starting transfers between devices  24.1 us (18%)
  local copies, waits for them, and re-layouts  5.81 us (4%)
  other arithmetic  3.61 us (3%)
    all_to_all x3, waiting for transfers between devices, exchange(): lax.all_to_all(array, 'expert', split_axis=0, concat_axis=0, tiled=True)  35.8 us
    all_to_all x3, starting transfers between devices, exchange(): lax.all_to_all(array, 'expert', split_axis=0, concat_axis=0, tiled=True)  23.6 us
    dot_general x4, matrix products, product(): lax.dot_general(part, columns, (((0,), (0,)), ((), ())), preferred_elemen...  22.6 us
    dot_general x1, matrix products, shards(): lax.dot_general(grad_rows, weight_out, (((1,), (1,)), ((), ())), preferre...  13.6 us
    dot_general x1, matrix products, shards(): pre = jnp.dot(received, weight_in, preferred_element_type=jnp.float32)  10.9 us
    dot_general x2, matrix products, fill_slots(): lax.dot_general(select, values, (((0,), (0,)), ((), ())), preferred_eleme...  6.66 us
    dot_general x1, matrix products, shards(): jnp.dot(hidden, weight_out, preferred_element_type=jnp.float32)  5.69 us
    dot_general x1, matrix products, shards(): expert_out = jnp.dot(select, back, preferred_element_type=jnp.float32)  4.01 us
  transfers between devices with their start and end apart: 5, of which 3 were waited for; matrix products, arithmetic and copies ran while one was open for 45% of the time, Pallas kernels for 0%

commit v1 on v0

--- a/solution.py
+++ b/solution.py
@@ -31,8 +31,9 @@
             part, columns, (((0,), (0,)), ((), ())), preferred_element_type=jnp.float32
         )
 
-    other = lax.ppermute(product(1 - here).astype(jnp.bfloat16), "replica", SWAP)
-    return product(here) + other.astype(jnp.float32)
+    share = product(1 - here).astype(jnp.bfloat16)
+    pieces = [lax.ppermute(piece, "replica", SWAP) for piece in jnp.split(share, 2, axis=0)]
+    return product(here) + jnp.concatenate(pieces, axis=0).astype(jnp.float32)
 
 
 def shards(tokens, expert_id, router_prob, keep_mask, w_in, w_out, cotangent):
@@ -56,9 +57,7 @@
         )
         return filled.astype(jnp.bfloat16).reshape(n_expert, capacity, width)
 
-    received = exchange(fill_slots(tokens)).reshape(slots, width)
     gated = (router_prob[:, None] * cotangent.astype(jnp.float32)).astype(jnp.bfloat16)
-    grad_rows = exchange(fill_slots(gated)).reshape(slots, width)
     keep_rows = lax.dynamic_index_in_dim(
         keep_mask[0].reshape(n_expert, n_replica, -1),
         lax.axis_index("replica"),
@@ -66,20 +65,27 @@
         keepdims=False,
     )
     keep_scale = keep_rows.astype(jnp.float32) * KEEP_SCALE
+    sent = fill_slots(tokens)
+    sent_grad = fill_slots(gated)
+    received = exchange(sent).reshape(slots, width)
+    sent_grad, keep_scale = lax.optimization_barrier((sent_grad, keep_scale))
+    grad_rows = exchange(sent_grad).reshape(slots, width)
     keep_scale = jnp.broadcast_to(keep_scale[:, None, :], (n_expert, capacity, keep_scale.shape[1]))
     keep_scale = keep_scale.reshape(slots, -1)
     pre = jnp.dot(received, weight_in, preferred_element_type=jnp.float32)
     value, slope = gelu_parts(pre)
     hidden = (value * keep_scale).astype(jnp.bfloat16)
-    slope = slope * keep_scale
+    slope = (slope * keep_scale).astype(jnp.bfloat16)
     out = jnp.dot(hidden, weight_out, preferred_element_type=jnp.float32).astype(jnp.bfloat16)
+    out, grad_rows = lax.optimization_barrier((out, grad_rows))
     back = exchange(out.reshape(n_expert, capacity, width)).reshape(slots, width)
     grad_out = summed_over_copies(hidden, grad_rows)
     dhidden = lax.dot_general(
         grad_rows, weight_out, (((1,), (1,)), ((), ())), preferred_element_type=jnp.float32
     )
-    dpre = (dhidden * slope).astype(jnp.bfloat16)
+    dpre = (dhidden * slope.astype(jnp.float32)).astype(jnp.bfloat16)
     grad_in = summed_over_copies(received, dpre)
+    back, grad_in, grad_out = lax.optimization_barrier((back, grad_in, grad_out))
     expert_out = jnp.dot(select, back, preferred_element_type=jnp.float32)
     mixed = (router_prob[:, None] * expert_out).astype(jnp.bfloat16)
     return (mixed, grad_in[None], grad_out[None])

time: 134 us -> 127 us (0.948)
  waiting for transfers between devices: 35.8 us -> 28.3 us
  matrix products: 63.5 us -> 59 us
  local copies, waits for them, and re-layouts: 5.81 us -> 8.73 us
    all_to_all x3, waiting for transfers between devices: 35.8 us -> 28.3 us  [exchange(): lax.all_to_all(array, 'expert', split_axis=0, concat_axis=0, tiled=True)]
    dot_general x1, matrix products: 13.6 us -> 8.74 us  [shards(): lax.dot_general(grad_rows, weight_out, (((1,), (1,)), ((), ())), preferre...]
    split x0 -> x2, local copies, waits for them, and re-layouts: none -> 2.97 us  [summed_over_copies(): jnp.split(share, 2, axis=0)]
    dot_general x1, matrix products: 10.9 us -> 12.6 us  [shards(): pre = jnp.dot(received, weight_in, preferred_element_type=jnp.float32)]
  transfers between devices with their start and end apart: 5 -> 7, of which waited for: 3 -> 2; matrix products, arithmetic and copies ran while one was open for 45% -> 49% of each run, Pallas kernels for 0% -> 0%
where the time goes in v1:
time: 127 us; the launch traced here: 125 us
  matrix products  59 us (46%)
  waiting for transfers between devices  28.3 us (22%)
  starting transfers between devices  24.9 us (20%)
  local copies, waits for them, and re-layouts  8.73 us (7%)
  other arithmetic  3.61 us (3%)
    all_to_all x3, waiting for transfers between devices, exchange(): lax.all_to_all(array, 'expert', split_axis=0, concat_axis=0, tiled=True)  28.3 us
    all_to_all x3, starting transfers between devices, exchange(): lax.all_to_all(array, 'expert', split_axis=0, concat_axis=0, tiled=True)  23.8 us
    dot_general x4, matrix products, product(): lax.dot_general(part, columns, (((0,), (0,)), ((), ())), preferred_elemen...  21.4 us
    dot_general x1, matrix products, shards(): pre = jnp.dot(received, weight_in, preferred_element_type=jnp.float32)  12.6 us
    dot_general x1, matrix products, shards(): lax.dot_general(grad_rows, weight_out, (((1,), (1,)), ((), ())), preferre...  8.74 us
    dot_general x2, matrix products, fill_slots(): lax.dot_general(select, values, (((0,), (0,)), ((), ())), preferred_eleme...  6.65 us
    dot_general x1, matrix products, shards(): jnp.dot(hidden, weight_out, preferred_element_type=jnp.float32)  5.75 us
    dot_general x1, matrix products, shards(): expert_out = jnp.dot(select, back, preferred_element_type=jnp.float32)  3.86 us
  transfers between devices with their start and end apart: 7, of which 2 were waited for; matrix products, arithmetic and copies ran while one was open for 49% of the time, Pallas kernels for 0%

profile of v1, /device:TPU:0, one launch (start us, length us, event | category | flops | bytes accessed | tf_op | source)
XLA Modules:
  0.0 125.3 jit_solution(11759612314987062061)
XLA Ops:
  0.6 1.0 convert_reduce_fusion
  1.7 0.7 multiply_add_fusion.1
  2.4 2.7 %fusion.21 = bf16[1024,1024]{1,0:T(8,128)(2,1)} fusion(bf16[512,1024]{1,0:T(8,128)(2,1)S(1)} %copy-done, s32[512]{0:T(512)S(1)} %bitcast.52), kind=kOutput, calls=%fused_computation.30 | convolution fusion | flops 1075314688 | bytes 3147776 | tf_op jit(solution)/shard_map/dot_general | solution.py:55
  5.1 11.6 %all-to-all-start = ((bf16[64,16,1024]{2,1,0:T(8,128)(2,1)}), bf16[64,16,1024]{2,1,0:T(8,128)(2,1)S(1)}, u32[]{:S(2)}, u32[]{:S(2)}) async-start(bf16[64,16,1024]{2,1,0:T(8,128)(2,1)} %bitcast.48), calls=%async_computation | async-start | bytes 4194304 | tf_op jit(solution)/shard_map/all_to_all | solution.py:21
  16.7 2.8 %reshape_squeeze.3 = s32[64,2,2048]{2,1,0:T(2,128)} reshape(s32[1,128,2048]{2,1,0:T(8,128)} %param.10) | data formatting | bytes 2097152 | tf_op jit(solution)/shard_map/reshape;squeeze | solution.py:62
  19.5 1.9 %convert_multiply_fusion = f32[64,1,2048]{2,1,0:T(1,128)S(1)} fusion(s32[64,2,2048]{2,1,0:T(2,128)} %reshape_squeeze.3, s32[]{:T(128)S(6)} %select_n.16), kind=kLoop, calls=%fused_computation.45 | loop fusion | flops 262144 | bytes 1048580 | tf_op jit(solution)/shard_map/mul | solution.py:67
  21.4 1.0 copy.12
  22.4 4.0 %fusion.22 = bf16[1024,1024]{1,0:T(8,128)(2,1)} fusion(bf16[512,1024]{1,0:T(8,128)(2,1)} %param.13, s32[512]{0:T(512)S(1)} %bitcast.53, f32[512]{0:T(512)S(1)} %copy-done.4), kind=kOutput, calls=%fused_computation.31 | convolution fusion | flops 1076887552 | bytes 3149824 | tf_op jit(solution)/shard_map/dot_general | solution.py:55
  26.3 20.0 %all-to-all-done = bf16[64,16,1024]{2,1,0:T(8,128)(2,1)S(1)} async-done(((bf16[64,16,1024]{2,1,0:T(8,128)(2,1)}), bf16[64,16,1024]{2,1,0:T(8,128)(2,1)S(1)}, u32[]{:S(2)}, u32[]{:S(2)}) %all-to-all-start) | async-done | bytes 2097184 | tf_op jit(solution)/shard_map/all_to_all | solution.py:21
  46.3 5.8 %all-to-all-start.1 = ((bf16[64,16,1024]{2,1,0:T(8,128)(2,1)}), bf16[64,16,1024]{2,1,0:T(8,128)(2,1)}, u32[]{:S(2)}, u32[]{:S(2)}) async-start(bf16[64,16,1024]{2,1,0:T(8,128)(2,1)} %bitcast.47), calls=%async_computation.1 | async-start | bytes 4194304 | tf_op jit(solution)/shard_map/all_to_all | solution.py:21
  52.1 12.6 %fusion.6 = (bf16[1024,2048]{1,0:T(8,128)(2,1)}, bf16[1024,2048]{1,0:T(8,128)(2,1)S(1)}) fusion(f32[64,2048]{1,0:T(8,128)} %bitcast.49, bf16[1024,1024]{1,0:T(8,128)(2,1)S(1)} %bitcast.42, bf16[1,1024,2048]{2,1,0:T(8,128)(2,1)} %param.11), kind=kOutput, calls=%fused_computation.10 | convolution fusion | flops 4341104640 | bytes 15204352 | tf_op jit(solution)/shard_map/dot_general | solution.py:75
  64.7 2.0 %copy-done.5 = bf16[1024,2048]{1,0:T(8,128)(2,1)} copy-done((bf16[1024,2048]{1,0:T(8,128)(2,1)}, bf16[1024,2048]{1,0:T(8,128)(2,1)S(1)}, u32[]{:S(2)}) %copy-start.5) | copy-done | bytes 4194328
  66.7 5.8 %fusion.26 = bf16[1024,1024]{1,0:T(8,128)(2,1)} fusion(bf16[1024,2048]{1,0:T(8,128)(2,1)S(1)} %get-tuple-element.18, bf16[1,2048,1024]{2,1,0:T(8,128)(2,1)S(1)} %copy-done.3), kind=kOutput, calls=%fused_computation.33 | convolution fusion | flops 4296015872 | bytes 10485760 | tf_op jit(solution)/shard_map/dot_general | solution.py:79
  72.4 8.4 %all-to-all-done.1 = bf16[64,16,1024]{2,1,0:T(8,128)(2,1)} async-done(((bf16[64,16,1024]{2,1,0:T(8,128)(2,1)}), bf16[64,16,1024]{2,1,0:T(8,128)(2,1)}, u32[]{:S(2)}, u32[]{:S(2)}) %all-to-all-start.1) | async-done | bytes 2097184 | tf_op jit(solution)/shard_map/all_to_all | solution.py:21
  80.8 6.4 %all-to-all-start.2 = ((bf16[64,16,1024]{2,1,0:T(8,128)(2,1)}), bf16[64,16,1024]{2,1,0:T(8,128)(2,1)}, u32[]{:S(2)}, u32[]{:S(2)}) async-start(bf16[64,16,1024]{2,1,0:T(8,128)(2,1)} %bitcast.46), calls=%async_computation.2 | async-start | bytes 4194304 | tf_op jit(solution)/shard_map/all_to_all | solution.py:21
  87.2 8.7 %multiply_convert_fusion = bf16[1024,2048]{1,0:T(8,128)(2,1)S(1)} fusion(bf16[1024,2048]{1,0:T(8,128)(2,1)} %get-tuple-element.17, bf16[1024,1024]{1,0:T(8,128)(2,1)} %bitcast.9, bf16[1,2048,1024]{2,1,0:T(8,128)(2,1)} %param.12), kind=kOutput, calls=%fused_computation.11 | convolution fusion | flops 4301258752 | bytes 14680064 | tf_op jit(solution)/shard_map/dot_general | solution.py:83
  96.0 5.5 %fusion.23 = bf16[1024,1024]{1,0:T(8,128)(2,1)S(1)} fusion(bf16[1024,1024]{1,0:T(8,128)(2,1)} %bitcast.9, bf16[1024,2048]{1,0:T(8,128)(2,1)S(1)} %copy-done.6, s32[]{:T(128)S(6)} %select_n.20), kind=kOutput, calls=%fused_computation.32 | convolution fusion | flops 2148532224 | bytes 6291460 | tf_op jit(solution)/shard_map/dot_general | solution.py:30
  101.5 1.5 %fusion.43 = (bf16[512,1024]{1,0:T(8,128)(2,1)}, bf16[512,1024]{1,0:T(8,128)(2,1)}) fusion(bf16[1024,1024]{1,0:T(8,128)(2,1)S(1)} %fusion.23), kind=kLoop, calls=%fused_computation.51 | loop fusion | bytes 4194304 | tf_op jit(solution)/shard_map/split | solution.py:35
  103.1 0.5 collective-permute-start.3
  103.6 2.5 %convolution_convert_fusion = bf16[512,2048]{1,0:T(8,128)(2,1)S(1)} fusion(bf16[1024,2048]{1,0:T(8,128)(2,1)S(1)} %multiply_convert_fusion, bf16[1024,1024]{1,0:T(8,128)(2,1)S(1)} %bitcast.43, s32[]{:T(128)S(6)} %select_n.18), kind=kOutput, calls=%fused_computation.19 | convolution fusion | flops 2148532224 | bytes 7340036 | tf_op jit(solution)/shard_map/dot_general | solution.py:30
  106.0 1.5 %fusion.44 = (bf16[256,2048]{1,0:T(8,128)(2,1)}, bf16[256,2048]{1,0:T(8,128)(2,1)}) fusion(bf16[512,2048]{1,0:T(8,128)(2,1)S(1)} %convolution_convert_fusion), kind=kLoop, calls=%fused_computation.52 | loop fusion | bytes 4194304 | tf_op jit(solution)/shard_map/split | solution.py:35
  108.0 7.4 %convert_add_fusion = f32[1024,1024]{1,0:T(8,128)} fusion(bf16[512,1024]{1,0:T(8,128)(2,1)} %collective-permute-done.3, bf16[512,1024]{1,0:T(8,128)(2,1)} %collective-permute-done.2, bf16[1024,1024]{1,0:T(8,128)(2,1)} %bitcast.9, bf16[1024,2048]{1,0:T(8,128)(2,1)} %copy-done.5, s32[]{:T(128)S(6)} %select_n.19), kind=kOutput, calls=%fused_computation.17 | convolution fusion | flops 2152726528 | bytes 10485764 | tf_op jit(solution)/shard_map/dot_general | solution.py:30
  115.4 6.0 %convert_add_fusion.1 = f32[512,2048]{1,0:T(8,128)} fusion(bf16[256,2048]{1,0:T(8,128)(2,1)} %collective-permute-done.1, bf16[256,2048]{1,0:T(8,128)(2,1)} %collective-permute-done, bf16[1024,2048]{1,0:T(8,128)(2,1)S(1)} %copy-done.2, bf16[1024,1024]{1,0:T(8,128)(2,1)S(1)} %bitcast.44, s32[]{:T(128)S(6)} %select_n.17), kind=kOutput, calls=%fused_computation.18 | convolution fusion | flops 2152726528 | bytes 11534340 | tf_op jit(solution)/shard_map/dot_general | solution.py:30
  121.4 3.9 %multiply_convert_fusion.1 = bf16[512,1024]{1,0:T(8,128)(2,1)} fusion(bf16[1024,1024]{1,0:T(8,128)(2,1)} %bitcast.11, s32[512]{0:T(512)S(1)} %bitcast.54, f32[512]{0:T(512)S(1)} %copy-done.4), kind=kOutput, calls=%fused_computation.20 | convolution fusion | flops 1075314688 | bytes 3149824 | tf_op jit(solution)/shard_map/dot_general | solution.py:89
  (21 shorter events, 0.6 us)
Async XLA Ops:
  0.6 1.7 %copy-start = (bf16[512,1024]{1,0:T(8,128)(2,1)S(1)}, bf16[512,1024]{1,0:T(8,128)(2,1)}, u32[]{:S(2)}) copy-start(bf16[512,1024]{1,0:T(8,128)(2,1)} %param.7) | copy-start | bytes 3145732
  5.1 17.3 %copy-start.4 = (f32[512]{0:T(512)S(1)}, f32[512]{0:T(512)}, u32[]{:S(2)}) copy-start(f32[512]{0:T(512)} %param.9) | copy-start | bytes 6148
  5.1 41.2 %all-to-all-start = ((bf16[64,16,1024]{2,1,0:T(8,128)(2,1)}), bf16[64,16,1024]{2,1,0:T(8,128)(2,1)S(1)}, u32[]{:S(2)}, u32[]{:S(2)}) async-start(bf16[64,16,1024]{2,1,0:T(8,128)(2,1)} %bitcast.48), calls=%async_computation | async-start | bytes 4194304 | tf_op jit(solution)/shard_map/all_to_all | solution.py:21
  46.3 34.5 %all-to-all-start.1 = ((bf16[64,16,1024]{2,1,0:T(8,128)(2,1)}), bf16[64,16,1024]{2,1,0:T(8,128)(2,1)}, u32[]{:S(2)}, u32[]{:S(2)}) async-start(bf16[64,16,1024]{2,1,0:T(8,128)(2,1)} %bitcast.47), calls=%async_computation.1 | async-start | bytes 4194304 | tf_op jit(solution)/shard_map/all_to_all | solution.py:21
  52.1 14.6 %copy-start.3 = (bf16[1,2048,1024]{2,1,0:T(8,128)(2,1)S(1)}, bf16[1,2048,1024]{2,1,0:T(8,128)(2,1)}, u32[]{:S(2)}) copy-start(bf16[1,2048,1024]{2,1,0:T(8,128)(2,1)} %param.12) | copy-start | bytes 12582916
  64.7 2.0 %copy-start.5 = (bf16[1024,2048]{1,0:T(8,128)(2,1)}, bf16[1024,2048]{1,0:T(8,128)(2,1)S(1)}, u32[]{:S(2)}) copy-start(bf16[1024,2048]{1,0:T(8,128)(2,1)S(1)} %get-tuple-element.18) | copy-start | bytes 12582916
  80.8 40.6 %all-to-all-start.2 = ((bf16[64,16,1024]{2,1,0:T(8,128)(2,1)}), bf16[64,16,1024]{2,1,0:T(8,128)(2,1)}, u32[]{:S(2)}, u32[]{:S(2)}) async-start(bf16[64,16,1024]{2,1,0:T(8,128)(2,1)} %bitcast.46), calls=%async_computation.2 | async-start | bytes 4194304 | tf_op jit(solution)/shard_map/all_to_all | solution.py:21
  87.2 8.8 %copy-start.6 = (bf16[1024,2048]{1,0:T(8,128)(2,1)S(1)}, bf16[1024,2048]{1,0:T(8,128)(2,1)}, u32[]{:S(2)}) copy-start(bf16[1024,2048]{1,0:T(8,128)(2,1)} %copy-done.5) | copy-start | bytes 12582916
  96.0 7.6 %copy-start.1 = (bf16[1024,2048]{1,0:T(8,128)(2,1)}, bf16[1024,2048]{1,0:T(8,128)(2,1)S(1)}, u32[]{:S(2)}) copy-start(bf16[1024,2048]{1,0:T(8,128)(2,1)S(1)} %multiply_convert_fusion) | copy-start | bytes 12582916
  103.1 5.0 %collective-permute-start.2 = (bf16[512,1024]{1,0:T(8,128)(2,1)}, bf16[512,1024]{1,0:T(8,128)(2,1)}, u32[]{:S(2)}, u32[]{:S(2)}) collective-permute-start(bf16[512,1024]{1,0:T(8,128)(2,1)} %get-tuple-element.19), channel_id=1, source_target_pairs={{0,1},{1,0},{2,3},{3,2},{4,5},{5,4},{6,7},{7,6},{8,9},{9,8},{10,11... | collective-permute-start | bytes 3145736 | tf_op jit(solution)/shard_map/ppermute | solution.py:35
  103.1 5.0 %collective-permute-start.3 = (bf16[512,1024]{1,0:T(8,128)(2,1)}, bf16[512,1024]{1,0:T(8,128)(2,1)}, u32[]{:S(2)}, u32[]{:S(2)}) collective-permute-start(bf16[512,1024]{1,0:T(8,128)(2,1)} %get-tuple-element.20), channel_id=1, source_target_pairs={{0,1},{1,0},{2,3},{3,2},{4,5},{5,4},{6,7},{7,6},{8,9},{9,8},{10,11... | collective-permute-start | bytes 3145736 | tf_op jit(solution)/shard_map/ppermute | solution.py:35
  107.5 7.9 %collective-permute-start = (bf16[256,2048]{1,0:T(8,128)(2,1)}, bf16[256,2048]{1,0:T(8,128)(2,1)}, u32[]{:S(2)}, u32[]{:S(2)}) collective-permute-start(bf16[256,2048]{1,0:T(8,128)(2,1)} %get-tuple-element.21), channel_id=1, source_target_pairs={{0,1},{1,0},{2,3},{3,2},{4,5},{5,4},{6,7},{7,6},{8,9},{9,8},{10,11... | collective-permute-start | bytes 3145736 | tf_op jit(solution)/shard_map/ppermute | solution.py:35
  107.5 7.9 %collective-permute-start.1 = (bf16[256,2048]{1,0:T(8,128)(2,1)}, bf16[256,2048]{1,0:T(8,128)(2,1)}, u32[]{:S(2)}, u32[]{:S(2)}) collective-permute-start(bf16[256,2048]{1,0:T(8,128)(2,1)} %get-tuple-element.22), channel_id=1, source_target_pairs={{0,1},{1,0},{2,3},{3,2},{4,5},{5,4},{6,7},{7,6},{8,9},{9,8},{10,11... | collective-permute-start | bytes 3145736 | tf_op jit(solution)/shard_map/ppermute | solution.py:35
  108.0 7.4 %copy-start.2 = (bf16[1024,2048]{1,0:T(8,128)(2,1)S(1)}, bf16[1024,2048]{1,0:T(8,128)(2,1)}, u32[]{:S(2)}) copy-start(bf16[1024,2048]{1,0:T(8,128)(2,1)} %copy-done.1) | copy-start | bytes 12582916

commit v2 on v1

--- a/solution.py
+++ b/solution.py
@@ -1,10 +1,115 @@
+import functools
+
 import jax
 import jax.numpy as jnp
 from jax import lax
+from jax.experimental import pallas as pl
+from jax.experimental.pallas import tpu as pltpu
 from jax.sharding import PartitionSpec as P
 
 KEEP_SCALE = 4.0 / 3.0
 SWAP = [(0, 1), (1, 0)]
+TN = (((0,), (0,)), ((), ()))
+NT = (((1,), (1,)), ((), ()))
+CHUNKS = 4
+PARAMS = pltpu.CompilerParams(vmem_limit_bytes=16 * 2**20)
+VMEM = pl.BlockSpec(memory_space=pltpu.VMEM)
+SMEM = pl.BlockSpec(memory_space=pltpu.SMEM)
+
+
+def resident(array):
+    return pltpu.with_memory_space_constraint(array, pltpu.VMEM)
+
+
+def cut(ref, dim, index, count):
+    size = ref.shape[dim] // count
+    part = pl.ds(index * size, size)
+    return ref.at[part, :] if dim == 0 else ref.at[:, part]
+
+
+def half_of(ref, which):
+    half = ref.shape[1] // 2
+    return ref.at[:, pl.ds(pl.multiple_of(which * half, half), half)]
+
+
+def part_of_product(dim, c, rows, columns):
+    left, right = (cut(rows, 1, c, CHUNKS), columns) if dim == 0 else (rows, cut(columns, 1, c, CHUNKS))
+    return lax.dot_general(left[...], right[...], TN, preferred_element_type=jnp.float32)
+
+
+def far_kernel(dim, which_ref, rows, columns, *outs):
+    half = rows.shape[1] // 2
+    for c in range(CHUNKS):
+        total = part_of_product(dim, c, half_of(rows, which_ref[0]), columns)
+        cut(outs[c // 2], dim, c % 2, 2)[...] = total.astype(jnp.bfloat16)
+
+
+def near_kernel(dim, which_ref, rows, columns, first, second, out_hbm, out, sem):
+    departures = []
+    for c in range(CHUNKS):
+        far = cut((first, second)[c // 2], dim, c % 2, 2)
+        total = part_of_product(dim, c, half_of(rows, which_ref[0]), columns)
+        cut(out, dim, c, CHUNKS)[...] = total + far[...].astype(jnp.float32)
+        departure = pltpu.make_async_copy(
+            cut(out, dim, c, CHUNKS), cut(out_hbm, dim, c, CHUNKS), sem.at[c]
+        )
+        departure.start()
+        departures.append(departure)
+    for departure in departures:
+        departure.wait()
+
+
+def half_product(which, rows, columns, dim, far=None):
+    half, wide = rows.shape[1] // 2, columns.shape[1]
+    if far is None:
+        piece = (half // 2, wide) if dim == 0 else (half, wide // 2)
+        return pl.pallas_call(
+            functools.partial(far_kernel, dim),
+            out_shape=[pltpu.VMEM(piece, jnp.bfloat16)] * 2,
+            in_specs=[SMEM, VMEM, VMEM],
+            out_specs=[VMEM] * 2,
+            compiler_params=PARAMS,
+            name="far_product",
+        )(which, resident(rows), resident(columns))
+    return pl.pallas_call(
+        functools.partial(near_kernel, dim),
+        out_shape=jax.ShapeDtypeStruct((half, wide), jnp.float32),
+        in_specs=[SMEM] + [VMEM] * 4,
+        out_specs=pl.BlockSpec(memory_space=pl.ANY),
+        scratch_shapes=[
+            pltpu.VMEM((half, wide), jnp.float32),
+            pltpu.SemaphoreType.DMA((CHUNKS,)),
+        ],
+        compiler_params=PARAMS,
+        name="near_product",
+    )(which, resident(rows), resident(columns), resident(far[0]), resident(far[1]))
+
+
+def backward_kernel(which_ref, grads, weight, slope, rows, dpre, *far):
+    depth = grads.shape[0]
+    for c in range(CHUNKS):
+        for r in range(4):
+            dhidden = lax.dot_general(
+                cut(grads, 0, r, 4)[...], cut(weight, 0, c, CHUNKS)[...], NT, preferred_element_type=jnp.float32
+            )
+            factor = cut(cut(slope, 1, c, CHUNKS), 0, r, 4)[...].astype(jnp.float32)
+            cut(cut(dpre, 1, c, CHUNKS), 0, r, 4)[...] = (dhidden * factor).astype(jnp.bfloat16)
+        share = part_of_product(1, c, half_of(rows, which_ref[0]), dpre)
+        cut(far[c // 2], 1, c % 2, 2)[...] = share.astype(jnp.bfloat16)
+
+
+def backward(which, grads, weight, slope, rows):
+    depth, width = grads.shape
+    hidden, half = slope.shape[1], width // 2
+    piece = pltpu.VMEM((half, hidden // 2), jnp.bfloat16)
+    return pl.pallas_call(
+        backward_kernel,
+        out_shape=[pltpu.VMEM((depth, hidden), jnp.bfloat16), piece, piece],
+        in_specs=[SMEM] + [VMEM] * 4,
+        out_specs=[VMEM] * 3,
+        compiler_params=PARAMS,
+        name="backward",
+    )(which, *map(resident, (grads, weight, slope, rows)))
 
 
 def gelu_parts(pre):
@@ -21,19 +126,8 @@
     return lax.all_to_all(array, "expert", split_axis=0, concat_axis=0, tiled=True)
 
 
-def summed_over_copies(rows, columns):
-    half = rows.shape[1] // 2
-    here = lax.axis_index("replica")
-
-    def product(which):
-        part = lax.dynamic_slice_in_dim(rows, which * half, half, axis=1)
-        return lax.dot_general(
-            part, columns, (((0,), (0,)), ((), ())), preferred_element_type=jnp.float32
-        )
-
-    share = product(1 - here).astype(jnp.bfloat16)
-    pieces = [lax.ppermute(piece, "replica", SWAP) for piece in jnp.split(share, 2, axis=0)]
-    return product(here) + jnp.concatenate(pieces, axis=0).astype(jnp.float32)
+def swapped(pieces):
+    return [lax.ppermute(piece, "replica", SWAP) for piece in pieces]
 
 
 def shards(tokens, expert_id, router_prob, keep_mask, w_in, w_out, cotangent):
@@ -79,12 +173,13 @@
     out = jnp.dot(hidden, weight_out, preferred_element_type=jnp.float32).astype(jnp.bfloat16)
     out, grad_rows = lax.optimization_barrier((out, grad_rows))
     back = exchange(out.reshape(n_expert, capacity, width)).reshape(slots, width)
-    grad_out = summed_over_copies(hidden, grad_rows)
-    dhidden = lax.dot_general(
-        grad_rows, weight_out, (((1,), (1,)), ((), ())), preferred_element_type=jnp.float32
-    )
-    dpre = (dhidden * slope.astype(jnp.float32)).astype(jnp.bfloat16)
-    grad_in = summed_over_copies(received, dpre)
+    here = lax.axis_index("replica").reshape(1)
+    other = 1 - here
+    dpre, *far_in = backward(other, grad_rows, weight_out, slope, received)
+    far_in = swapped(far_in)
+    far_out = swapped(half_product(other, hidden, grad_rows, 0))
+    grad_in = half_product(here, received, dpre, 1, far_in)
+    grad_out = half_product(here, hidden, grad_rows, 0, far_out)
     back, grad_in, grad_out = lax.optimization_barrier((back, grad_in, grad_out))
     expert_out = jnp.dot(select, back, preferred_element_type=jnp.float32)
     mixed = (router_prob[:, None] * expert_out).astype(jnp.bfloat16)

time: 127 us -> 122 us (0.961); the launches traced: 125 us -> 122 us
  matrix products: 59 us -> 29.6 us
  Pallas kernels: 0 us -> 15.9 us
  waiting for transfers between devices: 28.3 us -> 35.6 us
  local copies, waits for them, and re-layouts: 8.73 us -> 11.7 us
    dot_general x5 -> x0, matrix products: 30.1 us -> none  [the longest x4 21.4 us: product(): lax.dot_general(part, columns, (((0,), (0,)), ((), ())), preferred_elemen...]
    pallas_call x0 -> x4, Pallas kernels: none -> 15.9 us  [the longest x1 6.78 us: backward(): pl.pallas_call(backward_kernel, out_shape=[pltpu.VMEM((depth, hidden), jn...]
    all_to_all x3, waiting for transfers between devices: 28.3 us -> 35.4 us  [exchange(): lax.all_to_all(array, 'expert', split_axis=0, concat_axis=0, tiled=True)]
    unnamed x15 -> x21, local copies, waits for them, and re-layouts: 2.95 us -> 8.87 us
    split x2 -> x0, local copies, waits for them, and re-layouts: 2.97 us -> none  [summed_over_copies(): jnp.split(share, 2, axis=0)]
  transfers between devices with their start and end apart: 7 -> 7, of which waited for: 2 -> 4; matrix products, arithmetic and copies ran while one was open for 49% -> 24% of each run, Pallas kernels for 0% -> 13%
where the time goes in v2:
time: 122 us
  waiting for transfers between devices  35.6 us (29%)
  matrix products  29.6 us (24%)
  starting transfers between devices  24.5 us (20%)
  Pallas kernels  15.9 us (13%)
  local copies, waits for them, and re-layouts  11.7 us (10%)
  other arithmetic  3.61 us (3%)
    all_to_all x3, waiting for transfers between devices, exchange(): lax.all_to_all(array, 'expert', split_axis=0, concat_axis=0, tiled=True)  35.4 us
    all_to_all x3, starting transfers between devices, exchange(): lax.all_to_all(array, 'expert', split_axis=0, concat_axis=0, tiled=True)  23.3 us
    dot_general x1, matrix products, shards(): pre = jnp.dot(received, weight_in, preferred_element_type=jnp.float32)  13.3 us
    unnamed x21, local copies, waits for them, and re-layouts  8.87 us
    pallas_call x1, Pallas kernels, backward(): pl.pallas_call(backward_kernel, out_shape=[pltpu.VMEM((depth, hidden), jn...  6.78 us
    pallas_call x2, Pallas kernels, half_product(): pl.pallas_call(functools.partial(near_kernel, dim), out_shape=jax.ShapeDt...  6.77 us
    dot_general x2, matrix products, fill_slots(): lax.dot_general(select, values, (((0,), (0,)), ((), ())), preferred_eleme...  6.65 us
    dot_general x1, matrix products, shards(): jnp.dot(hidden, weight_out, preferred_element_type=jnp.float32)  5.74 us
  transfers between devices with their start and end apart: 7, of which 4 were waited for; matrix products, arithmetic and copies ran while one was open for 24% of the time, Pallas kernels for 13%

profile of v2, /device:TPU:0, one launch (start us, length us, event | category | flops | bytes accessed | tf_op | source)
XLA Modules:
  0.0 121.7 jit_solution(13974118717651221593)
XLA Ops:
  0.6 1.0 convert_reduce_fusion
  1.7 0.7 multiply_add_fusion.1
  2.4 2.7 %fusion.12 = bf16[1024,1024]{1,0:T(8,128)(2,1)} fusion(bf16[512,1024]{1,0:T(8,128)(2,1)S(1)} %copy-done, s32[512]{0:T(512)S(1)} %bitcast.49), kind=kOutput, calls=%fused_computation.19 | convolution fusion | flops 1075314688 | bytes 3147776 | tf_op jit(solution)/shard_map/dot_general | solution.py:149
  5.1 11.6 %all-to-all-start = ((bf16[64,16,1024]{2,1,0:T(8,128)(2,1)}), bf16[64,16,1024]{2,1,0:T(8,128)(2,1)S(1)}, u32[]{:S(2)}, u32[]{:S(2)}) async-start(bf16[64,16,1024]{2,1,0:T(8,128)(2,1)} %bitcast.44), calls=%async_computation | async-start | bytes 4194304 | tf_op jit(solution)/shard_map/all_to_all | solution.py:126
  16.7 2.8 %reshape_squeeze.3 = s32[64,2,2048]{2,1,0:T(2,128)} reshape(s32[1,128,2048]{2,1,0:T(8,128)} %param.10) | data formatting | bytes 2097152 | tf_op jit(solution)/shard_map/reshape;squeeze | solution.py:156
  19.5 1.9 %convert_multiply_fusion = f32[64,1,2048]{2,1,0:T(1,128)S(1)} fusion(s32[64,2,2048]{2,1,0:T(2,128)} %reshape_squeeze.3, s32[]{:T(128)S(6)} %select_n.4), kind=kLoop, calls=%fused_computation.30 | loop fusion | flops 262144 | bytes 1048580 | tf_op jit(solution)/shard_map/mul | solution.py:161
  21.4 1.0 copy.12
  22.4 4.0 %fusion.13 = bf16[1024,1024]{1,0:T(8,128)(2,1)} fusion(bf16[512,1024]{1,0:T(8,128)(2,1)} %param.13, s32[512]{0:T(512)S(1)} %bitcast.50, f32[512]{0:T(512)S(1)} %copy-done.9), kind=kOutput, calls=%fused_computation.20 | convolution fusion | flops 1076887552 | bytes 3149824 | tf_op jit(solution)/shard_map/dot_general | solution.py:149
  26.3 20.0 %all-to-all-done = bf16[64,16,1024]{2,1,0:T(8,128)(2,1)S(1)} async-done(((bf16[64,16,1024]{2,1,0:T(8,128)(2,1)}), bf16[64,16,1024]{2,1,0:T(8,128)(2,1)S(1)}, u32[]{:S(2)}, u32[]{:S(2)}) %all-to-all-start) | async-done | bytes 2097184 | tf_op jit(solution)/shard_map/all_to_all | solution.py:126
  46.3 1.4 %copy-done.1 = bf16[64,16,1024]{2,1,0:T(8,128)(2,1)} copy-done((bf16[64,16,1024]{2,1,0:T(8,128)(2,1)}, bf16[64,16,1024]{2,1,0:T(8,128)(2,1)S(1)}, u32[]{:S(2)}) %copy-start.1) | copy-done | bytes 2097176
  47.7 5.5 %all-to-all-start.1 = ((bf16[64,16,1024]{2,1,0:T(8,128)(2,1)}), bf16[64,16,1024]{2,1,0:T(8,128)(2,1)S(1)}, u32[]{:S(2)}, u32[]{:S(2)}) async-start(bf16[64,16,1024]{2,1,0:T(8,128)(2,1)} %bitcast.45), calls=%async_computation.1 | async-start | bytes 4194304 | tf_op jit(solution)/shard_map/all_to_all | solution.py:126
  53.2 13.3 %fusion.6 = (bf16[1024,2048]{1,0:T(8,128)(2,1)}, bf16[1024,2048]{1,0:T(8,128)(2,1)S(1)}) fusion(f32[64,2048]{1,0:T(8,128)} %bitcast.46, bf16[1024,1024]{1,0:T(8,128)(2,1)} %bitcast.37, bf16[1,1024,2048]{2,1,0:T(8,128)(2,1)} %param.11), kind=kOutput, calls=%fused_computation.10 | convolution fusion | flops 4341104640 | bytes 15204352 | tf_op jit(solution)/shard_map/dot_general | solution.py:169
  66.5 5.7 %convolution_convert_fusion = bf16[1024,1024]{1,0:T(8,128)(2,1)} fusion(bf16[1024,2048]{1,0:T(8,128)(2,1)S(1)} %get-tuple-element.28.rows, bf16[1,2048,1024]{2,1,0:T(8,128)(2,1)S(1)} %copy-done.6), kind=kOutput, calls=%fused_computation.21 | convolution fusion | flops 4296015872 | bytes 10485760 | tf_op jit(solution)/shard_map/dot_general | solution.py:173
  72.2 2.0 %copy-done.3 = bf16[1024,2048]{1,0:T(8,128)(2,1)} copy-done((bf16[1024,2048]{1,0:T(8,128)(2,1)}, bf16[1024,2048]{1,0:T(8,128)(2,1)S(1)}, u32[]{:S(2)}) %copy-start.3) | copy-done | bytes 4194328
  74.3 7.8 %all-to-all-done.1 = bf16[64,16,1024]{2,1,0:T(8,128)(2,1)S(1)} async-done(((bf16[64,16,1024]{2,1,0:T(8,128)(2,1)}), bf16[64,16,1024]{2,1,0:T(8,128)(2,1)S(1)}, u32[]{:S(2)}, u32[]{:S(2)}) %all-to-all-start.1) | async-done | bytes 2097184 | tf_op jit(solution)/shard_map/all_to_all | solution.py:126
  82.0 6.2 %all-to-all-start.2 = ((bf16[64,16,1024]{2,1,0:T(8,128)(2,1)}), bf16[64,16,1024]{2,1,0:T(8,128)(2,1)}, u32[]{:S(2)}, u32[]{:S(2)}) async-start(bf16[64,16,1024]{2,1,0:T(8,128)(2,1)} %bitcast.43), calls=%async_computation.2 | async-start | bytes 4194304 | tf_op jit(solution)/shard_map/all_to_all | solution.py:126
  88.3 2.3 %copy-done.4 = bf16[1024,2048]{1,0:T(8,128)(2,1)S(1)} copy-done((bf16[1024,2048]{1,0:T(8,128)(2,1)S(1)}, bf16[1024,2048]{1,0:T(8,128)(2,1)}, u32[]{:S(2)}) %copy-start.4) | copy-done | bytes 4194328
  90.6 2.4 %far_product.1 = (bf16[512,1024]{1,0:T(8,128)(2,1)S(1)}, bf16[512,1024]{1,0:T(8,128)(2,1)S(1)}) custom-call(s32[1]{0:T(128)S(6)} %sub.6.which_ref, bf16[1024,2048]{1,0:T(8,128)(2,1)S(1)} %copy-done.4, bf16[1024,1024]{1,0:T(8,128)(2,1)S(1)} %bitcast.34), custom_call_target="tpu_custom_call" | custom-call | tf_op jit(solution)/shard_map/far_product/pallas_call | solution.py:66
  93.6 2.2 %copy-done.8 = bf16[1024,2048]{1,0:T(8,128)(2,1)S(1)} copy-done((bf16[1024,2048]{1,0:T(8,128)(2,1)S(1)}, bf16[1024,2048]{1,0:T(8,128)(2,1)}, u32[]{:S(2)}) %copy-start.8) | copy-done | bytes 4194328
  95.8 6.8 %backward.1 = (bf16[1024,2048]{1,0:T(8,128)(2,1)S(1)}, bf16[512,1024]{1,0:T(8,128)(2,1)S(1)}, bf16[512,1024]{1,0:T(8,128)(2,1)S(1)}) custom-call(s32[1]{0:T(128)S(6)} %sub.6.which_ref, bf16[1024,1024]{1,0:T(8,128)(2,1)S(1)} %bitcast.35, bf16[2048,1024]{1,0:T(8,128)(2,1)S(1)} %bitcast.40, bf16[1024,2048]{1,0:T(8,128)(2,1)S(1)} %copy-done.8, ...), custom_call_target="tpu_custom_call" | custom-call | tf_op jit(solution)/shard_map/backward/pallas_call | solution.py:105
  103.2 3.4 %near_product.3 = f32[1024,1024]{1,0:T(8,128)} custom-call(s32[1]{0:T(128)} %bitcast.12.which_ref, bf16[1024,2048]{1,0:T(8,128)(2,1)S(1)} %copy-done.5, bf16[1024,1024]{1,0:T(8,128)(2,1)S(1)} %bitcast.36, bf16[512,1024]{1,0:T(8,128)(2,1)S(1)} %collective-permute-done.2.first, bf16[512,1024]{1,0:T(8,128)(2,1)S(1)} %collective-permute-done.3.second), custom_call_target="tpu_custom_call" | custom-call | tf_op jit(solution)/shard_map/near_product/pallas_call | solution.py:74
  106.8 3.4 %near_product.2 = f32[512,2048]{1,0:T(8,128)} custom-call(s32[1]{0:T(128)} %bitcast.12.which_ref, bf16[1024,1024]{1,0:T(8,128)(2,1)S(1)} %bitcast.39, bf16[1024,2048]{1,0:T(8,128)(2,1)S(1)} %get-tuple-element.19.columns, bf16[512,1024]{1,0:T(8,128)(2,1)S(1)} %collective-permute-done.first, bf16[512,1024]{1,0:T(8,128)(2,1)S(1)} %collective-permute-done.1.second), custom_call_target="tpu_custom_call" | custom-call | tf_op jit(solution)/shard_map/near_product/pallas_call | solution.py:74
  110.2 7.6 %all-to-all-done.2 = bf16[64,16,1024]{2,1,0:T(8,128)(2,1)} async-done(((bf16[64,16,1024]{2,1,0:T(8,128)(2,1)}), bf16[64,16,1024]{2,1,0:T(8,128)(2,1)}, u32[]{:S(2)}, u32[]{:S(2)}) %all-to-all-start.2) | async-done | bytes 2097184 | tf_op jit(solution)/shard_map/all_to_all | solution.py:126
  117.8 3.9 %multiply_convert_fusion = bf16[512,1024]{1,0:T(8,128)(2,1)} fusion(bf16[1024,1024]{1,0:T(8,128)(2,1)} %bitcast.11, s32[512]{0:T(512)S(1)} %bitcast.51, f32[512]{0:T(512)S(1)} %copy-done.9), kind=kOutput, calls=%fused_computation.13 | convolution fusion | flops 1075314688 | bytes 3149824 | tf_op jit(solution)/shard_map/dot_general | solution.py:184
  (24 shorter events, 1.4 us)
Async XLA Ops:
  0.6 1.7 %copy-start = (bf16[512,1024]{1,0:T(8,128)(2,1)S(1)}, bf16[512,1024]{1,0:T(8,128)(2,1)}, u32[]{:S(2)}) copy-start(bf16[512,1024]{1,0:T(8,128)(2,1)} %param.7) | copy-start | bytes 3145732
  5.1 17.3 %copy-start.9 = (f32[512]{0:T(512)S(1)}, f32[512]{0:T(512)}, u32[]{:S(2)}) copy-start(f32[512]{0:T(512)} %param.9) | copy-start | bytes 6148
  5.1 41.2 %all-to-all-start = ((bf16[64,16,1024]{2,1,0:T(8,128)(2,1)}), bf16[64,16,1024]{2,1,0:T(8,128)(2,1)S(1)}, u32[]{:S(2)}, u32[]{:S(2)}) async-start(bf16[64,16,1024]{2,1,0:T(8,128)(2,1)} %bitcast.44), calls=%async_computation | async-start | bytes 4194304 | tf_op jit(solution)/shard_map/all_to_all | solution.py:126
  46.3 1.4 %copy-start.1 = (bf16[64,16,1024]{2,1,0:T(8,128)(2,1)}, bf16[64,16,1024]{2,1,0:T(8,128)(2,1)S(1)}, u32[]{:S(2)}) copy-start(bf16[64,16,1024]{2,1,0:T(8,128)(2,1)S(1)} %all-to-all-done) | copy-start | bytes 6291460
  47.7 34.4 %all-to-all-start.1 = ((bf16[64,16,1024]{2,1,0:T(8,128)(2,1)}), bf16[64,16,1024]{2,1,0:T(8,128)(2,1)S(1)}, u32[]{:S(2)}, u32[]{:S(2)}) async-start(bf16[64,16,1024]{2,1,0:T(8,128)(2,1)} %bitcast.45), calls=%async_computation.1 | async-start | bytes 4194304 | tf_op jit(solution)/shard_map/all_to_all | solution.py:126
  53.2 13.3 %copy-start.6 = (bf16[1,2048,1024]{2,1,0:T(8,128)(2,1)S(1)}, bf16[1,2048,1024]{2,1,0:T(8,128)(2,1)}, u32[]{:S(2)}) copy-start(bf16[1,2048,1024]{2,1,0:T(8,128)(2,1)} %param.12) | copy-start | bytes 12582916
  72.2 2.0 %copy-start.3 = (bf16[1024,2048]{1,0:T(8,128)(2,1)}, bf16[1024,2048]{1,0:T(8,128)(2,1)S(1)}, u32[]{:S(2)}) copy-start(bf16[1024,2048]{1,0:T(8,128)(2,1)S(1)} %get-tuple-element.28.rows) | copy-start | bytes 12582916
  82.0 35.8 %all-to-all-start.2 = ((bf16[64,16,1024]{2,1,0:T(8,128)(2,1)}), bf16[64,16,1024]{2,1,0:T(8,128)(2,1)}, u32[]{:S(2)}, u32[]{:S(2)}) async-start(bf16[64,16,1024]{2,1,0:T(8,128)(2,1)} %bitcast.43), calls=%async_computation.2 | async-start | bytes 4194304 | tf_op jit(solution)/shard_map/all_to_all | solution.py:126
  88.3 5.3 %copy-start.2 = (bf16[64,16,1024]{2,1,0:T(8,128)(2,1)S(1)}, bf16[64,16,1024]{2,1,0:T(8,128)(2,1)}, u32[]{:S(2)}) copy-start(bf16[64,16,1024]{2,1,0:T(8,128)(2,1)} %copy-done.1) | copy-start | bytes 6291460
  88.3 2.3 %copy-start.4 = (bf16[1024,2048]{1,0:T(8,128)(2,1)S(1)}, bf16[1024,2048]{1,0:T(8,128)(2,1)}, u32[]{:S(2)}) copy-start(bf16[1024,2048]{1,0:T(8,128)(2,1)} %copy-done.3) | copy-start | bytes 12582916
  90.6 3.0 %copy-start.7 = (bf16[1,2048,1024]{2,1,0:T(8,128)(2,1)S(1)}, bf16[1,2048,1024]{2,1,0:T(8,128)(2,1)}, u32[]{:S(2)}) copy-start(bf16[1,2048,1024]{2,1,0:T(8,128)(2,1)} %param.12) | copy-start | bytes 12582916
  93.0 10.2 %collective-permute-start.2 = (bf16[512,1024]{1,0:T(8,128)(2,1)S(1)}, bf16[512,1024]{1,0:T(8,128)(2,1)S(1)}, u32[]{:S(2)}, u32[]{:S(2)}) collective-permute-start(bf16[512,1024]{1,0:T(8,128)(2,1)S(1)} %get-tuple-element.22), channel_id=1, source_target_pairs={{0,1},{1,0},{2,3},{3,2},{4,5},{5,4},{6,7},{7,6},{8,9},{9,8},{10,11... | collective-permute-start | bytes 3145736 | tf_op jit(solution)/shard_map/ppermute | solution.py:130
  93.1 10.1 %collective-permute-start.3 = (bf16[512,1024]{1,0:T(8,128)(2,1)S(1)}, bf16[512,1024]{1,0:T(8,128)(2,1)S(1)}, u32[]{:S(2)}, u32[]{:S(2)}) collective-permute-start(bf16[512,1024]{1,0:T(8,128)(2,1)S(1)} %get-tuple-element.23), channel_id=1, source_target_pairs={{0,1},{1,0},{2,3},{3,2},{4,5},{5,4},{6,7},{7,6},{8,9},{9,8},{10,11... | collective-permute-start | bytes 3145736 | tf_op jit(solution)/shard_map/ppermute | solution.py:130
  93.6 2.2 %copy-start.8 = (bf16[1024,2048]{1,0:T(8,128)(2,1)S(1)}, bf16[1024,2048]{1,0:T(8,128)(2,1)}, u32[]{:S(2)}) copy-start(bf16[1024,2048]{1,0:T(8,128)(2,1)} %get-tuple-element.27.slope) | copy-start | bytes 12582916
  95.8 7.4 %copy-start.5 = (bf16[1024,2048]{1,0:T(8,128)(2,1)S(1)}, bf16[1024,2048]{1,0:T(8,128)(2,1)}, u32[]{:S(2)}) copy-start(bf16[1024,2048]{1,0:T(8,128)(2,1)} %copy-done.3) | copy-start | bytes 12582916
  102.6 4.0 %collective-permute-start = (bf16[512,1024]{1,0:T(8,128)(2,1)S(1)}, bf16[512,1024]{1,0:T(8,128)(2,1)S(1)}, u32[]{:S(2)}, u32[]{:S(2)}) collective-permute-start(bf16[512,1024]{1,0:T(8,128)(2,1)S(1)} %get-tuple-element.20), channel_id=1, source_target_pairs={{0,1},{1,0},{2,3},{3,2},{4,5},{5,4},{6,7},{7,6},{8,9},{9,8},{10,11... | collective-permute-start | bytes 3145736 | tf_op jit(solution)/shard_map/ppermute | solution.py:130
  102.9 3.9 %collective-permute-start.1 = (bf16[512,1024]{1,0:T(8,128)(2,1)S(1)}, bf16[512,1024]{1,0:T(8,128)(2,1)S(1)}, u32[]{:S(2)}, u32[]{:S(2)}) collective-permute-start(bf16[512,1024]{1,0:T(8,128)(2,1)S(1)} %get-tuple-element.21), channel_id=1, source_target_pairs={{0,1},{1,0},{2,3},{3,2},{4,5},{5,4},{6,7},{7,6},{8,9},{9,8},{10,11... | collective-permute-start | bytes 3145736 | tf_op jit(solution)/shard_map/ppermute | solution.py:130

commit v3 on v2

--- a/solution.py
+++ b/solution.py
@@ -14,11 +14,16 @@
 CHUNKS = 4
 PARAMS = pltpu.CompilerParams(vmem_limit_bytes=16 * 2**20)
 VMEM = pl.BlockSpec(memory_space=pltpu.VMEM)
+ANY = pl.BlockSpec(memory_space=pl.ANY)
 SMEM = pl.BlockSpec(memory_space=pltpu.SMEM)
 
 
 def resident(array):
     return pltpu.with_memory_space_constraint(array, pltpu.VMEM)
+
+
+def in_hbm(array):
+    return pltpu.with_memory_space_constraint(array, pltpu.HBM)
 
 
 def cut(ref, dim, index, count):
@@ -44,11 +49,17 @@
         cut(outs[c // 2], dim, c % 2, 2)[...] = total.astype(jnp.bfloat16)
 
 
-def near_kernel(dim, which_ref, rows, columns, first, second, out_hbm, out, sem):
+def near_kernel(dim, which_ref, rows, columns, first, second, out_hbm, out, sem, *held):
+    rows = half_of(rows, which_ref[0])
+    if dim == 1:
+        arrival = pltpu.make_async_copy(rows, held[0], held[1])
+        arrival.start()
+        rows = held[0]
+        arrival.wait()
     departures = []
     for c in range(CHUNKS):
         far = cut((first, second)[c // 2], dim, c % 2, 2)
-        total = part_of_product(dim, c, half_of(rows, which_ref[0]), columns)
+        total = part_of_product(dim, c, rows, columns)
         cut(out, dim, c, CHUNKS)[...] = total + far[...].astype(jnp.float32)
         departure = pltpu.make_async_copy(
             cut(out, dim, c, CHUNKS), cut(out_hbm, dim, c, CHUNKS), sem.at[c]
@@ -74,19 +85,22 @@
     return pl.pallas_call(
         functools.partial(near_kernel, dim),
         out_shape=jax.ShapeDtypeStruct((half, wide), jnp.float32),
-        in_specs=[SMEM] + [VMEM] * 4,
-        out_specs=pl.BlockSpec(memory_space=pl.ANY),
+        in_specs=[SMEM, VMEM if dim == 0 else ANY] + [VMEM] * 3,
+        out_specs=ANY,
         scratch_shapes=[
             pltpu.VMEM((half, wide), jnp.float32),
             pltpu.SemaphoreType.DMA((CHUNKS,)),
+            *([] if dim == 0 else [pltpu.VMEM((rows.shape[0], half), jnp.bfloat16), pltpu.SemaphoreType.DMA]),
         ],
         compiler_params=PARAMS,
         name="near_product",
-    )(which, resident(rows), resident(columns), resident(far[0]), resident(far[1]))
-
-
-def backward_kernel(which_ref, grads, weight, slope, rows, dpre, *far):
-    depth = grads.shape[0]
+    )(which, resident(rows) if dim == 0 else in_hbm(rows), resident(columns), resident(far[0]), resident(far[1]))
+
+
+def backward_kernel(which_ref, grads, weight, slope, rows_hbm, dpre, first, second, rows, sem):
+    far = (first, second)
+    arrival = pltpu.make_async_copy(half_of(rows_hbm, which_ref[0]), rows, sem)
+    arrival.start()
     for c in range(CHUNKS):
         for r in range(4):
             dhidden = lax.dot_general(
@@ -94,7 +108,9 @@
             )
             factor = cut(cut(slope, 1, c, CHUNKS), 0, r, 4)[...].astype(jnp.float32)
             cut(cut(dpre, 1, c, CHUNKS), 0, r, 4)[...] = (dhidden * factor).astype(jnp.bfloat16)
-        share = part_of_product(1, c, half_of(rows, which_ref[0]), dpre)
+        if c == 0:
+            arrival.wait()
+        share = part_of_product(1, c, rows, dpre)
         cut(far[c // 2], 1, c % 2, 2)[...] = share.astype(jnp.bfloat16)
 
 
@@ -105,11 +121,100 @@
     return pl.pallas_call(
         backward_kernel,
         out_shape=[pltpu.VMEM((depth, hidden), jnp.bfloat16), piece, piece],
-        in_specs=[SMEM] + [VMEM] * 4,
+        in_specs=[SMEM] + [VMEM] * 3 + [ANY],
         out_specs=[VMEM] * 3,
+        scratch_shapes=[pltpu.VMEM((depth, half), jnp.bfloat16), pltpu.SemaphoreType.DMA],
         compiler_params=PARAMS,
         name="backward",
-    )(which, *map(resident, (grads, weight, slope, rows)))
+    )(which, *map(resident, (grads, weight, slope)), in_hbm(rows))
+
+
+def route_kernel(
+    experts, capacity, ids_hbm, tokens_hbm, target_ref, sent_hbm, named, tokens, sent, in_sem, out_sem
+):
+    naming = pltpu.make_async_copy(ids_hbm, named, in_sem.at[0])
+    naming.start()
+    arrival = pltpu.make_async_copy(tokens_hbm, tokens, in_sem.at[1])
+    arrival.start()
+    naming.wait()
+    ids = named[...]
+    count = ids.shape[1]
+    chosen = lax.broadcasted_iota(jnp.int32, (experts, count), 0) == ids
+    chosen = jnp.where(chosen, 1.0, 0.0)
+    earlier = lax.broadcasted_iota(jnp.int32, (count, count), 0) < lax.broadcasted_iota(
+        jnp.int32, (count, count), 1
+    )
+    earlier = jnp.where(earlier, 1.0, 0.0).astype(jnp.bfloat16)
+    ahead = jnp.dot(chosen.astype(jnp.bfloat16), earlier, preferred_element_type=jnp.float32)
+    rank = jnp.sum(chosen * ahead, axis=0, keepdims=True)
+    target = ids * capacity + rank.astype(jnp.int32)
+    target_ref[...] = target
+    arrival.wait()
+    size = sent.shape[0] // CHUNKS
+    departures = []
+    for c in range(CHUNKS):
+        row = lax.broadcasted_iota(jnp.int32, (size, count), 0) + c * size
+        select = jnp.where(row == target, 1.0, 0.0).astype(jnp.bfloat16)
+        filled = jnp.dot(select, tokens[...], preferred_element_type=jnp.float32)
+        cut(sent, 0, c, CHUNKS)[...] = filled.astype(jnp.bfloat16)
+        departure = pltpu.make_async_copy(
+            cut(sent, 0, c, CHUNKS), cut(sent_hbm, 0, c, CHUNKS), out_sem.at[c]
+        )
+        departure.start()
+        departures.append(departure)
+    for departure in departures:
+        departure.wait()
+
+
+def route(ids, tokens, experts, capacity):
+    filled = (experts * capacity, tokens.shape[1])
+    return pl.pallas_call(
+        functools.partial(route_kernel, experts, capacity),
+        out_shape=[
+            jax.ShapeDtypeStruct(ids.shape, jnp.int32),
+            pltpu.HBM(filled, jnp.bfloat16),
+        ],
+        in_specs=[ANY, ANY],
+        out_specs=[VMEM, ANY],
+        scratch_shapes=[
+            pltpu.VMEM(ids.shape, jnp.int32),
+            pltpu.VMEM(tokens.shape, jnp.bfloat16),
+            pltpu.VMEM(filled, jnp.bfloat16),
+            pltpu.SemaphoreType.DMA((2,)),
+            pltpu.SemaphoreType.DMA((CHUNKS,)),
+        ],
+        compiler_params=PARAMS,
+        name="route",
+    )(in_hbm(ids), in_hbm(tokens))
+
+
+def mix_kernel(target_ref, prob_ref, back_ref, mixed_hbm, mixed, sem):
+    slots, count = back_ref.shape[0], mixed.shape[0] // 2
+    departures = []
+    for c in range(2):
+        tokens = pl.ds(c * count, count)
+        slot = lax.broadcasted_iota(jnp.int32, (count, slots), 1)
+        select = jnp.where(slot == target_ref[tokens, :1], 1.0, 0.0).astype(jnp.bfloat16)
+        out = jnp.dot(select, back_ref[...], preferred_element_type=jnp.float32)
+        mixed[tokens, :] = (prob_ref[tokens, :1] * out).astype(jnp.bfloat16)
+        departure = pltpu.make_async_copy(mixed.at[tokens, :], mixed_hbm.at[tokens, :], sem.at[c])
+        departure.start()
+        departures.append(departure)
+    for departure in departures:
+        departure.wait()
+
+
+def mix(target, prob, back):
+    shape = (target.shape[0], back.shape[1])
+    return pl.pallas_call(
+        mix_kernel,
+        out_shape=jax.ShapeDtypeStruct(shape, jnp.bfloat16),
+        in_specs=[VMEM] * 3,
+        out_specs=ANY,
+        scratch_shapes=[pltpu.VMEM(shape, jnp.bfloat16), pltpu.SemaphoreType.DMA((2,))],
+        compiler_params=PARAMS,
+        name="mix",
+    )(resident(target), resident(prob), resident(back))
 
 
 def gelu_parts(pre):
@@ -138,19 +243,9 @@
     slots = n_expert * capacity
     weight_in = w_in[0]
     weight_out = w_out[0]
-    ids = expert_id[:, 0]
-    order = jnp.arange(tok_rows, dtype=jnp.int32)
-    earlier = (ids[:, None] == ids[None, :]) & (order[None, :] < order[:, None])
-    ranks = jnp.sum(earlier.astype(jnp.int32), axis=1)
-    target = ids * capacity + ranks
-    select = (target[:, None] == jnp.arange(slots, dtype=jnp.int32)[None, :]).astype(jnp.bfloat16)
-
-    def fill_slots(values):
-        filled = lax.dot_general(
-            select, values, (((0,), (0,)), ((), ())), preferred_element_type=jnp.float32
-        )
-        return filled.astype(jnp.bfloat16).reshape(n_expert, capacity, width)
-
+    ids = expert_id.reshape(1, tok_rows)
+    target, sent = route(ids, tokens, n_expert, capacity)
+    sent = sent.reshape(n_expert, capacity, width)
     gated = (router_prob[:, None] * cotangent.astype(jnp.float32)).astype(jnp.bfloat16)
     keep_rows = lax.dynamic_index_in_dim(
         keep_mask[0].reshape(n_expert, n_replica, -1),
@@ -159,10 +254,15 @@
         keepdims=False,
     )
     keep_scale = keep_rows.astype(jnp.float32) * KEEP_SCALE
-    sent = fill_slots(tokens)
-    sent_grad = fill_slots(gated)
+    select = jnp.arange(slots, dtype=jnp.int32)[:, None] == target
+    sent_grad = jnp.dot(select.astype(jnp.bfloat16), gated, preferred_element_type=jnp.float32)
+    sent_grad = sent_grad.astype(jnp.bfloat16).reshape(n_expert, capacity, width)
+    prob = jnp.broadcast_to(router_prob[:, None], (tok_rows, 128))
+    column = jnp.broadcast_to(target.reshape(tok_rows, 1), (tok_rows, 128))
     received = exchange(sent).reshape(slots, width)
-    sent_grad, keep_scale = lax.optimization_barrier((sent_grad, keep_scale))
+    sent_grad, keep_scale, prob, column = lax.optimization_barrier(
+        (sent_grad, keep_scale, prob, column)
+    )
     grad_rows = exchange(sent_grad).reshape(slots, width)
     keep_scale = jnp.broadcast_to(keep_scale[:, None, :], (n_expert, capacity, keep_scale.shape[1]))
     keep_scale = keep_scale.reshape(slots, -1)
@@ -181,8 +281,7 @@
     grad_in = half_product(here, received, dpre, 1, far_in)
     grad_out = half_product(here, hidden, grad_rows, 0, far_out)
     back, grad_in, grad_out = lax.optimization_barrier((back, grad_in, grad_out))
-    expert_out = jnp.dot(select, back, preferred_element_type=jnp.float32)
-    mixed = (router_prob[:, None] * expert_out).astype(jnp.bfloat16)
+    mixed = mix(column, prob, back)
     return (mixed, grad_in[None], grad_out[None])
 
 

time: 122 us -> 120 us (0.984)
  Pallas kernels: 15.9 us -> 24.6 us
  matrix products: 29.6 us -> 22.8 us
  local copies, waits for them, and re-layouts: 11.7 us -> 7.44 us
  other arithmetic: 3.61 us -> 0.67 us
  waiting for transfers between devices: 35.6 us -> 38.2 us
    pallas_call x0 -> x2, Pallas kernels: none -> 7.15 us  [the longest x1 3.71 us: mix(): pl.pallas_call(mix_kernel, out_shape=jax.ShapeDtypeStruct(shape, jnp.bflo...]
    dot_general x3 -> x1, matrix products: 10.5 us -> 3.93 us  [shards(): jnp.dot(select.astype(jnp.bfloat16), gated, preferred_element_type=jnp.fl...]
    all_to_all x3, waiting for transfers between devices: 35.4 us -> 38 us  [exchange(): lax.all_to_all(array, 'expert', split_axis=0, concat_axis=0, tiled=True)]
    unnamed x21 -> x17, local copies, waits for them, and re-layouts: 8.87 us -> 6.57 us
    another operation x1, local copies, waits for them, and re-layouts: 2.81 us -> 0.62 us  [shards(): keep_mask[0].reshape(n_expert, n_replica, -1)]
  transfers between devices with their start and end apart: 7 -> 7, of which waited for: 4 -> 4; matrix products, arithmetic and copies ran while one was open for 24% -> 21% of each run, Pallas kernels for 13% -> 15%
where the time goes in v3:
time: 120 us; the launch traced here: 119 us
  waiting for transfers between devices  38.2 us (32%)
  starting transfers between devices  24.7 us (21%)
  Pallas kernels  24.6 us (20%)
  matrix products  22.8 us (19%)
  local copies, waits for them, and re-layouts  7.44 us (6%)
    all_to_all x3, waiting for transfers between devices, exchange(): lax.all_to_all(array, 'expert', split_axis=0, concat_axis=0, tiled=True)  38 us
    all_to_all x3, starting transfers between devices, exchange(): lax.all_to_all(array, 'expert', split_axis=0, concat_axis=0, tiled=True)  23.5 us
    dot_general x1, matrix products, shards(): pre = jnp.dot(received, weight_in, preferred_element_type=jnp.float32)  13.2 us
    pallas_call x2, Pallas kernels, half_product(): pl.pallas_call(functools.partial(near_kernel, dim), out_shape=jax.ShapeDt...  7.99 us
    pallas_call x1, Pallas kernels, backward(): pl.pallas_call(backward_kernel, out_shape=[pltpu.VMEM((depth, hidden), jn...  7.07 us
    unnamed x17, local copies, waits for them, and re-layouts  6.57 us
    dot_general x1, matrix products, shards(): jnp.dot(hidden, weight_out, preferred_element_type=jnp.float32)  5.68 us
    dot_general x1, matrix products, shards(): jnp.dot(select.astype(jnp.bfloat16), gated, preferred_element_type=jnp.fl...  3.93 us
  transfers between devices with their start and end apart: 7, of which 4 were waited for; matrix products, arithmetic and copies ran while one was open for 21% of the time, Pallas kernels for 15%

profile of v3, /device:TPU:0, one launch (start us, length us, event | category | flops | bytes accessed | tf_op | source)
XLA Modules:
  0.0 119.4 jit_solution(10608632515072774754)
XLA Ops:
  0.6 3.4 %route.1 = (s32[1,512]{1,0:T(1,128)S(1)}, bf16[1024,1024]{1,0:T(8,128)(2,1)}) custom-call(s32[1,512]{1,0:T(1,128)} %bitcast.43, bf16[512,1024]{1,0:T(8,128)(2,1)} %tokens_hbm.1), custom_call_target="tpu_custom_call" | custom-call | tf_op jit(solution)/shard_map/route/pallas_call | solution.py:171
  4.1 11.8 %all-to-all-start = ((bf16[64,16,1024]{2,1,0:T(8,128)(2,1)}), bf16[64,16,1024]{2,1,0:T(8,128)(2,1)}, u32[]{:S(2)}, u32[]{:S(2)}) async-start(bf16[64,16,1024]{2,1,0:T(8,128)(2,1)} %bitcast.40), calls=%async_computation | async-start | bytes 4194304 | tf_op jit(solution)/shard_map/all_to_all | solution.py:231
  15.9 0.6 reshape_squeeze.3
  16.5 0.7 convert_multiply_fusion
  17.4 3.9 %fusion.10 = bf16[1024,1024]{1,0:T(8,128)(2,1)} fusion(bf16[512,1024]{1,0:T(8,128)(2,1)} %param.13, f32[512]{0:T(512)S(1)} %copy-done.7, s32[512]{0:T(512)S(1)} %bitcast.35), kind=kOutput, calls=%fused_computation.16 | convolution fusion | flops 1076887552 | bytes 3149824 | tf_op jit(solution)/shard_map/dot_general | solution.py:258
  21.6 23.8 %all-to-all-done = bf16[64,16,1024]{2,1,0:T(8,128)(2,1)} async-done(((bf16[64,16,1024]{2,1,0:T(8,128)(2,1)}), bf16[64,16,1024]{2,1,0:T(8,128)(2,1)}, u32[]{:S(2)}, u32[]{:S(2)}) %all-to-all-start) | async-done | bytes 2097184 | tf_op jit(solution)/shard_map/all_to_all | solution.py:231
  45.3 5.5 %all-to-all-start.1 = ((bf16[64,16,1024]{2,1,0:T(8,128)(2,1)}), bf16[64,16,1024]{2,1,0:T(8,128)(2,1)S(1)}, u32[]{:S(2)}, u32[]{:S(2)}) async-start(bf16[64,16,1024]{2,1,0:T(8,128)(2,1)} %bitcast.41), calls=%async_computation.1 | async-start | bytes 4194304 | tf_op jit(solution)/shard_map/all_to_all | solution.py:231
  50.8 13.2 %fusion.6 = (bf16[1024,2048]{1,0:T(8,128)(2,1)}, bf16[1024,2048]{1,0:T(8,128)(2,1)S(1)}) fusion(f32[64,2048]{1,0:T(8,128)S(1)} %bitcast.42, bf16[1024,1024]{1,0:T(8,128)(2,1)} %bitcast.4.rows_hbm.rows, bf16[1,1024,2048]{2,1,0:T(8,128)(2,1)} %param.11), kind=kOutput, calls=%fused_computation.10 | convolution fusion | flops 4341104640 | bytes 15204352 | tf_op jit(solution)/shard_map/dot_general | solution.py:269
  64.1 5.7 %convolution_convert_fusion = bf16[1024,1024]{1,0:T(8,128)(2,1)} fusion(bf16[1024,2048]{1,0:T(8,128)(2,1)S(1)} %get-tuple-element.36.rows, bf16[1,2048,1024]{2,1,0:T(8,128)(2,1)S(1)} %copy-done.3), kind=kOutput, calls=%fused_computation.17 | convolution fusion | flops 4296015872 | bytes 10485760 | tf_op jit(solution)/shard_map/dot_general | solution.py:273
  69.8 2.0 %copy-done = bf16[1024,2048]{1,0:T(8,128)(2,1)} copy-done((bf16[1024,2048]{1,0:T(8,128)(2,1)}, bf16[1024,2048]{1,0:T(8,128)(2,1)S(1)}, u32[]{:S(2)}) %copy-start) | copy-done | bytes 4194328
  71.8 7.9 %all-to-all-done.1 = bf16[64,16,1024]{2,1,0:T(8,128)(2,1)S(1)} async-done(((bf16[64,16,1024]{2,1,0:T(8,128)(2,1)}), bf16[64,16,1024]{2,1,0:T(8,128)(2,1)S(1)}, u32[]{:S(2)}, u32[]{:S(2)}) %all-to-all-start.1) | async-done | bytes 2097184 | tf_op jit(solution)/shard_map/all_to_all | solution.py:231
  79.7 6.2 %all-to-all-start.2 = ((bf16[64,16,1024]{2,1,0:T(8,128)(2,1)}), bf16[64,16,1024]{2,1,0:T(8,128)(2,1)}, u32[]{:S(2)}, u32[]{:S(2)}) async-start(bf16[64,16,1024]{2,1,0:T(8,128)(2,1)} %bitcast.39), calls=%async_computation.2 | async-start | bytes 4194304 | tf_op jit(solution)/shard_map/all_to_all | solution.py:231
  86.0 2.2 %copy-done.1 = bf16[1024,2048]{1,0:T(8,128)(2,1)S(1)} copy-done((bf16[1024,2048]{1,0:T(8,128)(2,1)S(1)}, bf16[1024,2048]{1,0:T(8,128)(2,1)}, u32[]{:S(2)}) %copy-start.1) | copy-done | bytes 4194328
  88.1 2.4 %far_product.1 = (bf16[512,1024]{1,0:T(8,128)(2,1)S(1)}, bf16[512,1024]{1,0:T(8,128)(2,1)S(1)}) custom-call(s32[1]{0:T(128)S(6)} %sub.6.which_ref, bf16[1024,2048]{1,0:T(8,128)(2,1)S(1)} %copy-done.1, bf16[1024,1024]{1,0:T(8,128)(2,1)S(1)} %bitcast.31), custom_call_target="tpu_custom_call" | custom-call | tf_op jit(solution)/shard_map/far_product/pallas_call | solution.py:77
  90.6 0.5 collective-permute-start.3
  91.1 2.2 %copy-done.5 = bf16[1024,2048]{1,0:T(8,128)(2,1)S(1)} copy-done((bf16[1024,2048]{1,0:T(8,128)(2,1)S(1)}, bf16[1024,2048]{1,0:T(8,128)(2,1)}, u32[]{:S(2)}) %copy-start.5) | copy-done | bytes 4194328
  93.3 7.1 %backward.1 = (bf16[1024,2048]{1,0:T(8,128)(2,1)S(1)}, bf16[512,1024]{1,0:T(8,128)(2,1)S(1)}, bf16[512,1024]{1,0:T(8,128)(2,1)S(1)}) custom-call(s32[1]{0:T(128)S(6)} %sub.6.which_ref, bf16[1024,1024]{1,0:T(8,128)(2,1)S(1)} %bitcast.32, bf16[2048,1024]{1,0:T(8,128)(2,1)S(1)} %bitcast.34, bf16[1024,2048]{1,0:T(8,128)(2,1)S(1)} %copy-done.5, ...), custom_call_target="tpu_custom_call" | custom-call | tf_op jit(solution)/shard_map/backward/pallas_call | solution.py:121
  100.4 0.4 collective-permute-start
  100.8 0.2 collective-permute-start.1
  101.0 3.4 %near_product.3 = f32[1024,1024]{1,0:T(8,128)} custom-call(s32[1]{0:T(128)} %bitcast.11.which_ref, bf16[1024,2048]{1,0:T(8,128)(2,1)S(1)} %copy-done.2, bf16[1024,1024]{1,0:T(8,128)(2,1)S(1)} %bitcast.33, bf16[512,1024]{1,0:T(8,128)(2,1)S(1)} %collective-permute-done.2.first, bf16[512,1024]{1,0:T(8,128)(2,1)S(1)} %collective-permute-done.3.second), custom_call_target="tpu_custom_call" | custom-call | tf_op jit(solution)/shard_map/near_product/pallas_call | solution.py:85
  104.4 0.2 collective-permute-done.1.second
  104.6 4.6 %near_product.2 = f32[512,2048]{1,0:T(8,128)} custom-call(s32[1]{0:T(128)} %bitcast.11.which_ref, bf16[1024,1024]{1,0:T(8,128)(2,1)} %bitcast.4.rows_hbm.rows, bf16[1024,2048]{1,0:T(8,128)(2,1)S(1)} %get-tuple-element.27.columns, bf16[512,1024]{1,0:T(8,128)(2,1)S(1)} %collective-permute-done.first, bf16[512,1024]{1,0:T(8,128)(2,1)S(1)} %collective-permute-done.1.second), custom_call_target="tpu_custom_call" | custom-call | tf_op jit(solution)/shard_map/near_product/pallas_call | solution.py:85
  109.2 6.3 %all-to-all-done.2 = bf16[64,16,1024]{2,1,0:T(8,128)(2,1)} async-done(((bf16[64,16,1024]{2,1,0:T(8,128)(2,1)}), bf16[64,16,1024]{2,1,0:T(8,128)(2,1)}, u32[]{:S(2)}, u32[]{:S(2)}) %all-to-all-start.2) | async-done | bytes 2097184 | tf_op jit(solution)/shard_map/all_to_all | solution.py:231
  115.5 3.7 %mix.1 = bf16[512,1024]{1,0:T(8,128)(2,1)} custom-call(s32[512,128]{1,0:T(8,128)S(1)} %broadcast_in_dim.11.target_ref, f32[512,128]{1,0:T(8,128)S(1)} %broadcast_in_dim.10.prob_ref, bf16[1024,1024]{1,0:T(8,128)(2,1)} %bitcast.10.back_ref), custom_call_target="tpu_custom_call" | custom-call | tf_op jit(solution)/shard_map/mix/pallas_call | solution.py:209
  (20 shorter events, 0.5 us)
Async XLA Ops:
  0.6 15.3 %copy-start.6 = (s32[1,128,2048]{2,1,0:T(8,128)S(1)}, s32[1,128,2048]{2,1,0:T(8,128)}, u32[]{:S(2)}) copy-start(s32[1,128,2048]{2,1,0:T(8,128)} %param.10) | copy-start | bytes 3145732
  4.1 13.3 %copy-start.7 = (f32[512]{0:T(512)S(1)}, f32[512]{0:T(512)}, u32[]{:S(2)}) copy-start(f32[512]{0:T(512)} %param.9) | copy-start | bytes 6148
  4.1 41.2 %all-to-all-start = ((bf16[64,16,1024]{2,1,0:T(8,128)(2,1)}), bf16[64,16,1024]{2,1,0:T(8,128)(2,1)}, u32[]{:S(2)}, u32[]{:S(2)}) async-start(bf16[64,16,1024]{2,1,0:T(8,128)(2,1)} %bitcast.40), calls=%async_computation | async-start | bytes 4194304 | tf_op jit(solution)/shard_map/all_to_all | solution.py:231
  45.3 34.4 %all-to-all-start.1 = ((bf16[64,16,1024]{2,1,0:T(8,128)(2,1)}), bf16[64,16,1024]{2,1,0:T(8,128)(2,1)S(1)}, u32[]{:S(2)}, u32[]{:S(2)}) async-start(bf16[64,16,1024]{2,1,0:T(8,128)(2,1)} %bitcast.41), calls=%async_computation.1 | async-start | bytes 4194304 | tf_op jit(solution)/shard_map/all_to_all | solution.py:231
  50.8 13.2 %copy-start.3 = (bf16[1,2048,1024]{2,1,0:T(8,128)(2,1)S(1)}, bf16[1,2048,1024]{2,1,0:T(8,128)(2,1)}, u32[]{:S(2)}) copy-start(bf16[1,2048,1024]{2,1,0:T(8,128)(2,1)} %param.12) | copy-start | bytes 12582916
  69.8 2.0 %copy-start = (bf16[1024,2048]{1,0:T(8,128)(2,1)}, bf16[1024,2048]{1,0:T(8,128)(2,1)S(1)}, u32[]{:S(2)}) copy-start(bf16[1024,2048]{1,0:T(8,128)(2,1)S(1)} %get-tuple-element.36.rows) | copy-start | bytes 12582916
  79.7 35.8 %all-to-all-start.2 = ((bf16[64,16,1024]{2,1,0:T(8,128)(2,1)}), bf16[64,16,1024]{2,1,0:T(8,128)(2,1)}, u32[]{:S(2)}, u32[]{:S(2)}) async-start(bf16[64,16,1024]{2,1,0:T(8,128)(2,1)} %bitcast.39), calls=%async_computation.2 | async-start | bytes 4194304 | tf_op jit(solution)/shard_map/all_to_all | solution.py:231
  85.9 2.2 %copy-start.1 = (bf16[1024,2048]{1,0:T(8,128)(2,1)S(1)}, bf16[1024,2048]{1,0:T(8,128)(2,1)}, u32[]{:S(2)}) copy-start(bf16[1024,2048]{1,0:T(8,128)(2,1)} %copy-done) | copy-start | bytes 12582916
  88.1 3.0 %copy-start.4 = (bf16[1,2048,1024]{2,1,0:T(8,128)(2,1)S(1)}, bf16[1,2048,1024]{2,1,0:T(8,128)(2,1)}, u32[]{:S(2)}) copy-start(bf16[1,2048,1024]{2,1,0:T(8,128)(2,1)} %param.12) | copy-start | bytes 12582916
  90.5 10.5 %collective-permute-start.2 = (bf16[512,1024]{1,0:T(8,128)(2,1)S(1)}, bf16[512,1024]{1,0:T(8,128)(2,1)S(1)}, u32[]{:S(2)}, u32[]{:S(2)}) collective-permute-start(bf16[512,1024]{1,0:T(8,128)(2,1)S(1)} %get-tuple-element.30), channel_id=1, source_target_pairs={{0,1},{1,0},{2,3},{3,2},{4,5},{5,4},{6,7},{7,6},{8,9},{9,8},{10,11... | collective-permute-start | bytes 3145736 | tf_op jit(solution)/shard_map/ppermute | solution.py:235
  90.6 10.4 %collective-permute-start.3 = (bf16[512,1024]{1,0:T(8,128)(2,1)S(1)}, bf16[512,1024]{1,0:T(8,128)(2,1)S(1)}, u32[]{:S(2)}, u32[]{:S(2)}) collective-permute-start(bf16[512,1024]{1,0:T(8,128)(2,1)S(1)} %get-tuple-element.31), channel_id=1, source_target_pairs={{0,1},{1,0},{2,3},{3,2},{4,5},{5,4},{6,7},{7,6},{8,9},{9,8},{10,11... | collective-permute-start | bytes 3145736 | tf_op jit(solution)/shard_map/ppermute | solution.py:235
  91.1 2.2 %copy-start.5 = (bf16[1024,2048]{1,0:T(8,128)(2,1)S(1)}, bf16[1024,2048]{1,0:T(8,128)(2,1)}, u32[]{:S(2)}) copy-start(bf16[1024,2048]{1,0:T(8,128)(2,1)} %get-tuple-element.35.slope) | copy-start | bytes 12582916
  93.3 7.7 %copy-start.2 = (bf16[1024,2048]{1,0:T(8,128)(2,1)S(1)}, bf16[1024,2048]{1,0:T(8,128)(2,1)}, u32[]{:S(2)}) copy-start(bf16[1024,2048]{1,0:T(8,128)(2,1)} %copy-done) | copy-start | bytes 12582916
  100.4 4.0 %collective-permute-start = (bf16[512,1024]{1,0:T(8,128)(2,1)S(1)}, bf16[512,1024]{1,0:T(8,128)(2,1)S(1)}, u32[]{:S(2)}, u32[]{:S(2)}) collective-permute-start(bf16[512,1024]{1,0:T(8,128)(2,1)S(1)} %get-tuple-element.28), channel_id=1, source_target_pairs={{0,1},{1,0},{2,3},{3,2},{4,5},{5,4},{6,7},{7,6},{8,9},{9,8},{10,11... | collective-permute-start | bytes 3145736 | tf_op jit(solution)/shard_map/ppermute | solution.py:235
  100.8 3.9 %collective-permute-start.1 = (bf16[512,1024]{1,0:T(8,128)(2,1)S(1)}, bf16[512,1024]{1,0:T(8,128)(2,1)S(1)}, u32[]{:S(2)}, u32[]{:S(2)}) collective-permute-start(bf16[512,1024]{1,0:T(8,128)(2,1)S(1)} %get-tuple-element.29), channel_id=1, source_target_pairs={{0,1},{1,0},{2,3},{3,2},{4,5},{5,4},{6,7},{7,6},{8,9},{9,8},{10,11... | collective-permute-start | bytes 3145736 | tf_op jit(solution)/shard_map/ppermute | solution.py:235

commit v4 on v3

--- a/solution.py
+++ b/solution.py
@@ -188,33 +188,35 @@
     )(in_hbm(ids), in_hbm(tokens))
 
 
-def mix_kernel(target_ref, prob_ref, back_ref, mixed_hbm, mixed, sem):
-    slots, count = back_ref.shape[0], mixed.shape[0] // 2
-    departures = []
-    for c in range(2):
-        tokens = pl.ds(c * count, count)
-        slot = lax.broadcasted_iota(jnp.int32, (count, slots), 1)
-        select = jnp.where(slot == target_ref[tokens, :1], 1.0, 0.0).astype(jnp.bfloat16)
-        out = jnp.dot(select, back_ref[...], preferred_element_type=jnp.float32)
-        mixed[tokens, :] = (prob_ref[tokens, :1] * out).astype(jnp.bfloat16)
-        departure = pltpu.make_async_copy(mixed.at[tokens, :], mixed_hbm.at[tokens, :], sem.at[c])
-        departure.start()
-        departures.append(departure)
-    for departure in departures:
-        departure.wait()
+def mix_kernel(target_ref, prob_ref, back_hbm, mixed_ref, back, in_sem):
+    parts = 2
+    count = back.shape[0] // parts
+    arrivals = [
+        pltpu.make_async_copy(cut(back_hbm, 0, c, parts), cut(back, 0, c, parts), in_sem.at[c])
+        for c in range(parts)
+    ]
+    for arrival in arrivals:
+        arrival.start()
+    total = None
+    for c in range(parts):
+        slot = lax.broadcasted_iota(jnp.int32, (mixed_ref.shape[0], count), 1) + c * count
+        select = jnp.where(slot == target_ref[:, :1], 1.0, 0.0).astype(jnp.bfloat16)
+        arrivals[c].wait()
+        out = jnp.dot(select, cut(back, 0, c, parts)[...], preferred_element_type=jnp.float32)
+        total = out if total is None else total + out
+    mixed_ref[...] = (prob_ref[:, :1] * total).astype(jnp.bfloat16)
 
 
 def mix(target, prob, back):
-    shape = (target.shape[0], back.shape[1])
     return pl.pallas_call(
         mix_kernel,
-        out_shape=jax.ShapeDtypeStruct(shape, jnp.bfloat16),
-        in_specs=[VMEM] * 3,
-        out_specs=ANY,
-        scratch_shapes=[pltpu.VMEM(shape, jnp.bfloat16), pltpu.SemaphoreType.DMA((2,))],
+        out_shape=jax.ShapeDtypeStruct((target.shape[0], back.shape[1]), jnp.bfloat16),
+        in_specs=[VMEM, VMEM, ANY],
+        out_specs=VMEM,
+        scratch_shapes=[pltpu.VMEM(back.shape, jnp.bfloat16), pltpu.SemaphoreType.DMA((2,))],
         compiler_params=PARAMS,
         name="mix",
-    )(resident(target), resident(prob), resident(back))
+    )(resident(target), resident(prob), in_hbm(back))
 
 
 def gelu_parts(pre):

time: 120 us -> 120 us (level)
  no operation moved by 1% of the time
where the time goes in v4:
time: 120 us; the launch traced here: 119 us
  waiting for transfers between devices  38.2 us (32%)
  Pallas kernels  24.7 us (21%)
  starting transfers between devices  24.7 us (21%)
  matrix products  22.8 us (19%)
  local copies, waits for them, and re-layouts  7.44 us (6%)
    all_to_all x3, waiting for transfers between devices, exchange(): lax.all_to_all(array, 'expert', split_axis=0, concat_axis=0, tiled=True)  38 us
    all_to_all x3, starting transfers between devices, exchange(): lax.all_to_all(array, 'expert', split_axis=0, concat_axis=0, tiled=True)  23.5 us
    dot_general x1, matrix products, shards(): pre = jnp.dot(received, weight_in, preferred_element_type=jnp.float32)  13.2 us
    pallas_call x2, Pallas kernels, half_product(): pl.pallas_call(functools.partial(near_kernel, dim), out_shape=jax.ShapeDt...  7.99 us
    pallas_call x1, Pallas kernels, backward(): pl.pallas_call(backward_kernel, out_shape=[pltpu.VMEM((depth, hidden), jn...  7.07 us
    unnamed x17, local copies, waits for them, and re-layouts  6.57 us
    dot_general x1, matrix products, shards(): jnp.dot(hidden, weight_out, preferred_element_type=jnp.float32)  5.68 us
    dot_general x1, matrix products, shards(): jnp.dot(select.astype(jnp.bfloat16), gated, preferred_element_type=jnp.fl...  3.93 us
  transfers between devices with their start and end apart: 7, of which 4 were waited for; matrix products, arithmetic and copies ran while one was open for 21% of the time, Pallas kernels for 15%

profile of v4, /device:TPU:0, one launch (start us, length us, event | category | flops | bytes accessed | tf_op | source)
XLA Modules:
  0.0 119.5 jit_solution(838374926057310277)
XLA Ops:
  0.6 3.4 %route.1 = (s32[1,512]{1,0:T(1,128)S(1)}, bf16[1024,1024]{1,0:T(8,128)(2,1)}) custom-call(s32[1,512]{1,0:T(1,128)} %bitcast.43, bf16[512,1024]{1,0:T(8,128)(2,1)} %tokens_hbm.1), custom_call_target="tpu_custom_call" | custom-call | tf_op jit(solution)/shard_map/route/pallas_call | solution.py:171
  4.1 11.8 %all-to-all-start = ((bf16[64,16,1024]{2,1,0:T(8,128)(2,1)}), bf16[64,16,1024]{2,1,0:T(8,128)(2,1)}, u32[]{:S(2)}, u32[]{:S(2)}) async-start(bf16[64,16,1024]{2,1,0:T(8,128)(2,1)} %bitcast.40), calls=%async_computation | async-start | bytes 4194304 | tf_op jit(solution)/shard_map/all_to_all | solution.py:233
  15.9 0.6 reshape_squeeze.3
  16.5 0.7 convert_multiply_fusion
  17.4 3.9 %fusion.10 = bf16[1024,1024]{1,0:T(8,128)(2,1)} fusion(bf16[512,1024]{1,0:T(8,128)(2,1)} %param.13, f32[512]{0:T(512)S(1)} %copy-done.7, s32[512]{0:T(512)S(1)} %bitcast.35), kind=kOutput, calls=%fused_computation.16 | convolution fusion | flops 1076887552 | bytes 3149824 | tf_op jit(solution)/shard_map/dot_general | solution.py:260
  21.6 23.8 %all-to-all-done = bf16[64,16,1024]{2,1,0:T(8,128)(2,1)} async-done(((bf16[64,16,1024]{2,1,0:T(8,128)(2,1)}), bf16[64,16,1024]{2,1,0:T(8,128)(2,1)}, u32[]{:S(2)}, u32[]{:S(2)}) %all-to-all-start) | async-done | bytes 2097184 | tf_op jit(solution)/shard_map/all_to_all | solution.py:233
  45.3 5.5 %all-to-all-start.1 = ((bf16[64,16,1024]{2,1,0:T(8,128)(2,1)}), bf16[64,16,1024]{2,1,0:T(8,128)(2,1)S(1)}, u32[]{:S(2)}, u32[]{:S(2)}) async-start(bf16[64,16,1024]{2,1,0:T(8,128)(2,1)} %bitcast.41), calls=%async_computation.1 | async-start | bytes 4194304 | tf_op jit(solution)/shard_map/all_to_all | solution.py:233
  50.8 13.2 %fusion.6 = (bf16[1024,2048]{1,0:T(8,128)(2,1)}, bf16[1024,2048]{1,0:T(8,128)(2,1)S(1)}) fusion(f32[64,2048]{1,0:T(8,128)S(1)} %bitcast.42, bf16[1024,1024]{1,0:T(8,128)(2,1)} %bitcast.4.rows_hbm.rows, bf16[1,1024,2048]{2,1,0:T(8,128)(2,1)} %param.11), kind=kOutput, calls=%fused_computation.10 | convolution fusion | flops 4341104640 | bytes 15204352 | tf_op jit(solution)/shard_map/dot_general | solution.py:271
  64.1 5.7 %convolution_convert_fusion = bf16[1024,1024]{1,0:T(8,128)(2,1)} fusion(bf16[1024,2048]{1,0:T(8,128)(2,1)S(1)} %get-tuple-element.36.rows, bf16[1,2048,1024]{2,1,0:T(8,128)(2,1)S(1)} %copy-done.3), kind=kOutput, calls=%fused_computation.17 | convolution fusion | flops 4296015872 | bytes 10485760 | tf_op jit(solution)/shard_map/dot_general | solution.py:275
  69.8 2.0 %copy-done = bf16[1024,2048]{1,0:T(8,128)(2,1)} copy-done((bf16[1024,2048]{1,0:T(8,128)(2,1)}, bf16[1024,2048]{1,0:T(8,128)(2,1)S(1)}, u32[]{:S(2)}) %copy-start) | copy-done | bytes 4194328
  71.8 7.9 %all-to-all-done.1 = bf16[64,16,1024]{2,1,0:T(8,128)(2,1)S(1)} async-done(((bf16[64,16,1024]{2,1,0:T(8,128)(2,1)}), bf16[64,16,1024]{2,1,0:T(8,128)(2,1)S(1)}, u32[]{:S(2)}, u32[]{:S(2)}) %all-to-all-start.1) | async-done | bytes 2097184 | tf_op jit(solution)/shard_map/all_to_all | solution.py:233
  79.7 6.2 %all-to-all-start.2 = ((bf16[64,16,1024]{2,1,0:T(8,128)(2,1)}), bf16[64,16,1024]{2,1,0:T(8,128)(2,1)}, u32[]{:S(2)}, u32[]{:S(2)}) async-start(bf16[64,16,1024]{2,1,0:T(8,128)(2,1)} %bitcast.39), calls=%async_computation.2 | async-start | bytes 4194304 | tf_op jit(solution)/shard_map/all_to_all | solution.py:233
  86.0 2.2 %copy-done.1 = bf16[1024,2048]{1,0:T(8,128)(2,1)S(1)} copy-done((bf16[1024,2048]{1,0:T(8,128)(2,1)S(1)}, bf16[1024,2048]{1,0:T(8,128)(2,1)}, u32[]{:S(2)}) %copy-start.1) | copy-done | bytes 4194328
  88.1 2.4 %far_product.1 = (bf16[512,1024]{1,0:T(8,128)(2,1)S(1)}, bf16[512,1024]{1,0:T(8,128)(2,1)S(1)}) custom-call(s32[1]{0:T(128)S(6)} %sub.6.which_ref, bf16[1024,2048]{1,0:T(8,128)(2,1)S(1)} %copy-done.1, bf16[1024,1024]{1,0:T(8,128)(2,1)S(1)} %bitcast.31), custom_call_target="tpu_custom_call" | custom-call | tf_op jit(solution)/shard_map/far_product/pallas_call | solution.py:77
  90.6 0.5 collective-permute-start.3
  91.1 2.2 %copy-done.5 = bf16[1024,2048]{1,0:T(8,128)(2,1)S(1)} copy-done((bf16[1024,2048]{1,0:T(8,128)(2,1)S(1)}, bf16[1024,2048]{1,0:T(8,128)(2,1)}, u32[]{:S(2)}) %copy-start.5) | copy-done | bytes 4194328
  93.3 7.1 %backward.1 = (bf16[1024,2048]{1,0:T(8,128)(2,1)S(1)}, bf16[512,1024]{1,0:T(8,128)(2,1)S(1)}, bf16[512,1024]{1,0:T(8,128)(2,1)S(1)}) custom-call(s32[1]{0:T(128)S(6)} %sub.6.which_ref, bf16[1024,1024]{1,0:T(8,128)(2,1)S(1)} %bitcast.32, bf16[2048,1024]{1,0:T(8,128)(2,1)S(1)} %bitcast.34, bf16[1024,2048]{1,0:T(8,128)(2,1)S(1)} %copy-done.5, ...), custom_call_target="tpu_custom_call" | custom-call | tf_op jit(solution)/shard_map/backward/pallas_call | solution.py:121
  100.4 0.4 collective-permute-start
  100.8 0.2 collective-permute-start.1
  101.0 3.4 %near_product.3 = f32[1024,1024]{1,0:T(8,128)} custom-call(s32[1]{0:T(128)} %bitcast.11.which_ref, bf16[1024,2048]{1,0:T(8,128)(2,1)S(1)} %copy-done.2, bf16[1024,1024]{1,0:T(8,128)(2,1)S(1)} %bitcast.33, bf16[512,1024]{1,0:T(8,128)(2,1)S(1)} %collective-permute-done.2.first, bf16[512,1024]{1,0:T(8,128)(2,1)S(1)} %collective-permute-done.3.second), custom_call_target="tpu_custom_call" | custom-call | tf_op jit(solution)/shard_map/near_product/pallas_call | solution.py:85
  104.4 0.2 collective-permute-done.1.second
  104.6 4.6 %near_product.2 = f32[512,2048]{1,0:T(8,128)} custom-call(s32[1]{0:T(128)} %bitcast.11.which_ref, bf16[1024,1024]{1,0:T(8,128)(2,1)} %bitcast.4.rows_hbm.rows, bf16[1024,2048]{1,0:T(8,128)(2,1)S(1)} %get-tuple-element.27.columns, bf16[512,1024]{1,0:T(8,128)(2,1)S(1)} %collective-permute-done.first, bf16[512,1024]{1,0:T(8,128)(2,1)S(1)} %collective-permute-done.1.second), custom_call_target="tpu_custom_call" | custom-call | tf_op jit(solution)/shard_map/near_product/pallas_call | solution.py:85
  109.2 6.3 %all-to-all-done.2 = bf16[64,16,1024]{2,1,0:T(8,128)(2,1)} async-done(((bf16[64,16,1024]{2,1,0:T(8,128)(2,1)}), bf16[64,16,1024]{2,1,0:T(8,128)(2,1)}, u32[]{:S(2)}, u32[]{:S(2)}) %all-to-all-start.2) | async-done | bytes 2097184 | tf_op jit(solution)/shard_map/all_to_all | solution.py:233
  115.5 3.8 %mix.1 = bf16[512,1024]{1,0:T(8,128)(2,1)} custom-call(s32[512,128]{1,0:T(8,128)S(1)} %broadcast_in_dim.11.target_ref, f32[512,128]{1,0:T(8,128)S(1)} %broadcast_in_dim.10.prob_ref, bf16[1024,1024]{1,0:T(8,128)(2,1)} %bitcast.10.back_hbm), custom_call_target="tpu_custom_call" | custom-call | tf_op jit(solution)/shard_map/mix/pallas_call | solution.py:211
  (20 shorter events, 0.5 us)
Async XLA Ops:
  0.6 15.3 %copy-start.6 = (s32[1,128,2048]{2,1,0:T(8,128)S(1)}, s32[1,128,2048]{2,1,0:T(8,128)}, u32[]{:S(2)}) copy-start(s32[1,128,2048]{2,1,0:T(8,128)} %param.10) | copy-start | bytes 3145732
  4.1 13.3 %copy-start.7 = (f32[512]{0:T(512)S(1)}, f32[512]{0:T(512)}, u32[]{:S(2)}) copy-start(f32[512]{0:T(512)} %param.9) | copy-start | bytes 6148
  4.1 41.2 %all-to-all-start = ((bf16[64,16,1024]{2,1,0:T(8,128)(2,1)}), bf16[64,16,1024]{2,1,0:T(8,128)(2,1)}, u32[]{:S(2)}, u32[]{:S(2)}) async-start(bf16[64,16,1024]{2,1,0:T(8,128)(2,1)} %bitcast.40), calls=%async_computation | async-start | bytes 4194304 | tf_op jit(solution)/shard_map/all_to_all | solution.py:233
  45.3 34.4 %all-to-all-start.1 = ((bf16[64,16,1024]{2,1,0:T(8,128)(2,1)}), bf16[64,16,1024]{2,1,0:T(8,128)(2,1)S(1)}, u32[]{:S(2)}, u32[]{:S(2)}) async-start(bf16[64,16,1024]{2,1,0:T(8,128)(2,1)} %bitcast.41), calls=%async_computation.1 | async-start | bytes 4194304 | tf_op jit(solution)/shard_map/all_to_all | solution.py:233
  50.8 13.2 %copy-start.3 = (bf16[1,2048,1024]{2,1,0:T(8,128)(2,1)S(1)}, bf16[1,2048,1024]{2,1,0:T(8,128)(2,1)}, u32[]{:S(2)}) copy-start(bf16[1,2048,1024]{2,1,0:T(8,128)(2,1)} %param.12) | copy-start | bytes 12582916
  69.8 2.0 %copy-start = (bf16[1024,2048]{1,0:T(8,128)(2,1)}, bf16[1024,2048]{1,0:T(8,128)(2,1)S(1)}, u32[]{:S(2)}) copy-start(bf16[1024,2048]{1,0:T(8,128)(2,1)S(1)} %get-tuple-element.36.rows) | copy-start | bytes 12582916
  79.7 35.8 %all-to-all-start.2 = ((bf16[64,16,1024]{2,1,0:T(8,128)(2,1)}), bf16[64,16,1024]{2,1,0:T(8,128)(2,1)}, u32[]{:S(2)}, u32[]{:S(2)}) async-start(bf16[64,16,1024]{2,1,0:T(8,128)(2,1)} %bitcast.39), calls=%async_computation.2 | async-start | bytes 4194304 | tf_op jit(solution)/shard_map/all_to_all | solution.py:233
  85.9 2.2 %copy-start.1 = (bf16[1024,2048]{1,0:T(8,128)(2,1)S(1)}, bf16[1024,2048]{1,0:T(8,128)(2,1)}, u32[]{:S(2)}) copy-start(bf16[1024,2048]{1,0:T(8,128)(2,1)} %copy-done) | copy-start | bytes 12582916
  88.1 3.0 %copy-start.4 = (bf16[1,2048,1024]{2,1,0:T(8,128)(2,1)S(1)}, bf16[1,2048,1024]{2,1,0:T(8,128)(2,1)}, u32[]{:S(2)}) copy-start(bf16[1,2048,1024]{2,1,0:T(8,128)(2,1)} %param.12) | copy-start | bytes 12582916
  90.5 10.5 %collective-permute-start.2 = (bf16[512,1024]{1,0:T(8,128)(2,1)S(1)}, bf16[512,1024]{1,0:T(8,128)(2,1)S(1)}, u32[]{:S(2)}, u32[]{:S(2)}) collective-permute-start(bf16[512,1024]{1,0:T(8,128)(2,1)S(1)} %get-tuple-element.30), channel_id=1, source_target_pairs={{0,1},{1,0},{2,3},{3,2},{4,5},{5,4},{6,7},{7,6},{8,9},{9,8},{10,11... | collective-permute-start | bytes 3145736 | tf_op jit(solution)/shard_map/ppermute | solution.py:237
  90.6 10.4 %collective-permute-start.3 = (bf16[512,1024]{1,0:T(8,128)(2,1)S(1)}, bf16[512,1024]{1,0:T(8,128)(2,1)S(1)}, u32[]{:S(2)}, u32[]{:S(2)}) collective-permute-start(bf16[512,1024]{1,0:T(8,128)(2,1)S(1)} %get-tuple-element.31), channel_id=1, source_target_pairs={{0,1},{1,0},{2,3},{3,2},{4,5},{5,4},{6,7},{7,6},{8,9},{9,8},{10,11... | collective-permute-start | bytes 3145736 | tf_op jit(solution)/shard_map/ppermute | solution.py:237
  91.1 2.2 %copy-start.5 = (bf16[1024,2048]{1,0:T(8,128)(2,1)S(1)}, bf16[1024,2048]{1,0:T(8,128)(2,1)}, u32[]{:S(2)}) copy-start(bf16[1024,2048]{1,0:T(8,128)(2,1)} %get-tuple-element.35.slope) | copy-start | bytes 12582916
  93.3 7.7 %copy-start.2 = (bf16[1024,2048]{1,0:T(8,128)(2,1)S(1)}, bf16[1024,2048]{1,0:T(8,128)(2,1)}, u32[]{:S(2)}) copy-start(bf16[1024,2048]{1,0:T(8,128)(2,1)} %copy-done) | copy-start | bytes 12582916
  100.4 4.0 %collective-permute-start = (bf16[512,1024]{1,0:T(8,128)(2,1)S(1)}, bf16[512,1024]{1,0:T(8,128)(2,1)S(1)}, u32[]{:S(2)}, u32[]{:S(2)}) collective-permute-start(bf16[512,1024]{1,0:T(8,128)(2,1)S(1)} %get-tuple-element.28), channel_id=1, source_target_pairs={{0,1},{1,0},{2,3},{3,2},{4,5},{5,4},{6,7},{7,6},{8,9},{9,8},{10,11... | collective-permute-start | bytes 3145736 | tf_op jit(solution)/shard_map/ppermute | solution.py:237
  100.8 3.9 %collective-permute-start.1 = (bf16[512,1024]{1,0:T(8,128)(2,1)S(1)}, bf16[512,1024]{1,0:T(8,128)(2,1)S(1)}, u32[]{:S(2)}, u32[]{:S(2)}) collective-permute-start(bf16[512,1024]{1,0:T(8,128)(2,1)S(1)} %get-tuple-element.29), channel_id=1, source_target_pairs={{0,1},{1,0},{2,3},{3,2},{4,5},{5,4},{6,7},{7,6},{8,9},{9,8},{10,11... | collective-permute-start | bytes 3145736 | tf_op jit(solution)/shard_map/ppermute | solution.py:237
